TPU v7x, 256 devices: a whole 4x4x8 slice. The times are simulated.
256 devices in a mesh: dp: 4 (over x), expert: 64 (over z, y, core).
Axes of the slice: x: 4, y: 4, z: 8, core: 2. Of those that a mesh axis runs over, the one named last changes fastest.
Arguments:
- tokens: bfloat16 [32768, 7168], P(('dp', 'expert')), may hold values from -6 to 6
- cotangent: bfloat16 [32768, 7168], P(('dp', 'expert')), may hold values from -6 to 6
- route_ids: int32 [32768, 8], P(('dp', 'expert')), may hold values from 0 to 255, all different within a row; in each aligned block of 128 rows (0 to 127, 128 to 255, ...) at most 5 rows name the same one
- router_weights: float32 [32768, 8], P(('dp', 'expert')), may hold values from 0.05 to 0.3
- master: float32 [64, 7168, 384], P('expert', 'dp'), may hold values from -0.0625 to 0.0625
- accumulator: float32 [64, 3, 7168], P('expert', None, 'dp'), may hold values from 0.1 to 10
Outputs:
- output: bfloat16 [32768, 7168], P(('dp', 'expert'))
- input_grad: bfloat16 [32768, 7168], P(('dp', 'expert'))
- new_weights: bfloat16 [64, 7168, 384], P('expert', 'dp')
- accumulator_out: float32 [64, 3, 7168], P('expert', None, 'dp')
Inputs may be any that keep to these rules, and one draw needn't show every extreme that they name: `route_ids`: each row names distinct experts. In each aligned block of 128 rows (the rows of one device) no expert is named by more than 5 rows, a bound that some block reaches.
All inputs are finite; a program needn't handle non-finite values.
Results may differ from a plain program's by a relative error of at most 0.011.
Values may be sent and summed in bfloat16 or wider, within the bound.
No kernel may reach another device: no remote copies, remote signals or barrier semaphores. Data moves between devices by JAX's collectives and lax.ppermute only.
A program may use at most 128 MiB of HBM per device.

v0:
```python
import functools

import jax
import jax.numpy as jnp
from jax import lax
from jax.experimental import pallas as pl
from jax.experimental.pallas import tpu as pltpu
from jax.sharding import Mesh, PartitionSpec as P


N_X, N_Z, N_Y, N_C = 4, 8, 4, 2
CAP = 5
LEARN_RATE = 0.01
EPSILON = 1e-06
BF = jnp.bfloat16
F32 = jnp.float32
COST = 100
ROOM = 60
SHARE = 28
BLK = 256


def swap_core(a):
    return lax.ppermute(a, "c", [(0, 1), (1, 0)])


def swap(a, axis, bits):
    return lax.ppermute(a, axis, [(i, i ^ bits) for i in range(lax.axis_size(axis))])


def shift(a, axis, step):
    n = lax.axis_size(axis)
    return lax.ppermute(a, axis, [(i, (i + step) % n) for i in range(n)])


def after(value, *firsts):
    return lax.optimization_barrier((value, *firsts))[0]


def iota(shape, dim):
    return lax.broadcasted_iota(jnp.int32, shape, dim)


def params(mib, **kw):
    return pltpu.CompilerParams(vmem_limit_bytes=mib << 20, **kw)


def like(*shape, dtype=BF):
    return jax.ShapeDtypeStruct(shape, dtype)


def dot_nn(a, b):
    return jnp.dot(a, b, preferred_element_type=F32)


def dot_nt(a, b):
    return lax.dot_general(a, b, (((1,), (1,)), ((), ())), preferred_element_type=F32)


def dot_tn(a, b):
    return lax.dot_general(a, b, (((0,), (0,)), ((), ())), preferred_element_type=F32)


def cost(micros):
    return pl.CostEstimate(
        flops=micros * 10**9, bytes_accessed=micros * 10**6, transcendentals=0
    )


def select_kernel(scaled, with_tab, x_ref, ids_ref, w_ref, *refs):
    del x_ref
    segs, refs = refs[:N_X], refs[N_X:]
    send_ref, refs = refs[0], refs[1:]
    if with_tab:
        (out_tab, in_tab), refs = refs[:2], refs[2:]
    sel_ref, row_ref = refs
    tok = ids_ref.shape[0]
    packed = send_ref.shape[2]
    blocks = packed // CAP

    @pl.when(pl.program_id(0) == 0)
    def _():
        lane = iota((tok, 128), 1)
        named = jnp.zeros((tok, 128), F32)
        weight = jnp.zeros((tok, 128), F32)
        for k in range(ids_ref.shape[1]):
            hit = ids_ref[:, k : k + 1] == lane
            named = jnp.where(hit, 1.0, named)
            weight = jnp.where(hit, w_ref[:, k : k + 1], weight)
        earlier = jnp.where(iota((tok, tok), 1) < iota((tok, tok), 0), 1.0, 0.0).astype(BF)
        place = dot_nn(earlier, named.astype(BF))
        code = jnp.where(named > 0, place + 1.0, 0.0)
        code_t = code.T
        weight_t = weight.T
        r = iota((packed, 1), 0)
        slot = (r % CAP + 1).astype(F32)
        shape = (packed, blocks * tok)
        diag = iota(shape, 0) // CAP == iota(shape, 1) // tok
        for e in range(N_Z):
            block = pl.ds(e * packed, packed)
            picked = jnp.broadcast_to(code_t[e : e + 1, :], (packed, tok)) == slot
            ones = jnp.where(picked, 1.0, 0.0)
            wide = jnp.concatenate([ones] * blocks, axis=1)
            sel_ref[block, :] = jnp.where(diag, wide, 0.0).astype(BF)
            if scaled:
                part = jnp.where(picked, jnp.broadcast_to(weight_t[e : e + 1, :], (packed, tok)), 0.0)
                row_ref[block, :] = jnp.broadcast_to(jnp.sum(part, axis=1, keepdims=True), (packed, 128))
        if with_tab:
            total = N_Z * packed
            l = iota((128, total), 1)
            spread = jnp.where(l // packed == iota((128, total), 0), 1.0, 0.0).astype(BF)
            l = iota((tok, total), 1) % packed
            valid = (dot_nn(code.astype(BF), spread) == (l % CAP + 1).astype(F32)) & (l < blocks * CAP)
            in_tab[...] = jnp.where(valid, 1.0, 0.0).astype(BF)
            out_tab[...] = jnp.where(valid, dot_nn(weight.astype(BF), spread), 0.0).astype(BF)

    wide = jnp.concatenate([s[...] for s in segs], axis=1)
    stack = jnp.concatenate([wide[:, q * BLK : (q + 1) * BLK] for q in range(blocks)], axis=0)
    rows = dot_nn(sel_ref[...], stack)
    if scaled:
        rows = rows * row_ref[:, :1]
    send_ref[...] = rows.astype(BF).reshape(send_ref.shape)


def packed_rows(width):
    blocks = width // N_C // BLK
    return -(-blocks * CAP // 8) * 8


def select(x, ids, weights, data, scaled, with_tab):
    tok, width = data.shape
    seg = width // (N_X * N_C)
    packed = packed_rows(width)
    blocks = packed // CAP
    total = N_Z * packed
    seg_spec = lambda k: pl.BlockSpec(
        (tok, seg), lambda c, x: (0, lax.bitwise_xor(x[0], k) * N_C + c)
    )
    out_specs = [pl.BlockSpec((N_Z, 1, packed, BLK), lambda c, x: (0, c, 0, 0))]
    out_shape = [like(N_Z, N_C, packed, BLK)]
    if with_tab:
        out_specs += [pl.BlockSpec((tok, total), lambda c, x: (0, 0))] * 2
        out_shape += [like(tok, total)] * 2
    return pl.pallas_call(
        functools.partial(select_kernel, scaled, with_tab),
        grid_spec=pltpu.PrefetchScalarGridSpec(
            num_scalar_prefetch=1,
            grid=(N_C,),
            in_specs=[
                pl.BlockSpec(ids.shape, lambda c, x: (0, 0)),
                pl.BlockSpec(weights.shape, lambda c, x: (0, 0)),
            ]
            + [seg_spec(k) for k in range(N_X)],
            out_specs=out_specs,
            scratch_shapes=[
                pltpu.VMEM((total, blocks * tok), BF),
                pltpu.VMEM((total, 128), F32),
            ],
        ),
        out_shape=out_shape,
        compiler_params=params(SHARE),
        cost_estimate=cost(COST),
        name="select_cot" if scaled else "select_tok",
    )(x, ids, weights, *([data] * N_X))


GROWS = N_Z * CAP


def unpack_kernel(in_ref, out_ref):
    packed = in_ref.shape[1]
    blocks = packed // CAP
    shape = (blocks * GROWS, N_Z * packed)
    row, col = iota(shape, 0), iota(shape, 1)
    place = row % GROWS
    want = place // CAP * packed + row // GROWS * CAP + place % CAP
    perm = jnp.where(col == want, 1.0, 0.0).astype(BF)
    out = dot_nn(perm, in_ref[...].reshape(N_Z * packed, BLK))
    for q in range(blocks):
        out_ref[:, pl.ds(q * BLK, BLK)] = out[q * GROWS : (q + 1) * GROWS].astype(BF)


def unpack(packed):
    srcs, rows, _ = packed.shape
    width = rows // CAP * BLK
    return pl.pallas_call(
        unpack_kernel,
        grid=(srcs // N_Z,),
        in_specs=[pl.BlockSpec((N_Z, rows, BLK), lambda h: (h, 0, 0))],
        out_specs=pl.BlockSpec((GROWS, width), lambda h: (h, 0)),
        out_shape=like(srcs * CAP, width),
        compiler_params=params(SHARE),
        cost_estimate=cost(COST),
        name="unpack_rows",
    )(packed)


def pack_kernel(*refs):
    *parts, send_ref = refs
    packed = send_ref.shape[1]
    blocks = packed // CAP
    total = sum(r[...].astype(F32) for r in parts)
    stack = jnp.concatenate(
        [total[:, q * BLK : (q + 1) * BLK] for q in range(blocks)], axis=0
    ).astype(BF)
    shape = (N_Z * packed, blocks * GROWS)
    row, col = iota(shape, 0), iota(shape, 1)
    r = row % packed
    want = r // CAP * GROWS + row // packed * CAP + r % CAP
    perm = jnp.where((col == want) & (r < blocks * CAP), 1.0, 0.0).astype(BF)
    send_ref[...] = dot_nn(perm, stack).astype(BF).reshape(send_ref.shape)


def pack(*parts):
    rows, width = parts[0].shape
    packed = packed_rows(width * N_C)
    return pl.pallas_call(
        pack_kernel,
        grid=(rows // GROWS,),
        in_specs=[pl.BlockSpec((GROWS, width), lambda h: (h, 0))] * len(parts),
        out_specs=pl.BlockSpec((N_Z, packed, BLK), lambda h: (h, 0, 0)),
        out_shape=like(rows // CAP, packed, BLK),
        compiler_params=params(SHARE),
        cost_estimate=cost(COST),
        name="pack_rows",
    )(*parts)


GROUP = 7


def combine_kernel(x_ref, tab_ref, back_ref, out_ref, big_ref, acc_ref):
    del x_ref
    c, k = pl.program_id(0), pl.program_id(1)
    tok, total = tab_ref.shape
    packed = back_ref.shape[2]
    blocks = packed // CAP
    seg = out_ref.shape[1]

    @pl.when((c == 0) & (k == 0))
    def _():
        where = iota((tok, total), 1) % packed // CAP
        for q in range(blocks):
            big_ref[pl.ds(q * tok, tok), :] = jnp.where(where == q, tab_ref[...], jnp.zeros((), BF))

    @pl.when(k == 0)
    def _():
        back = back_ref[...].reshape(total, BLK)

        def block(i, carry):
            span = pl.ds(pl.multiple_of(i * GROUP * tok, tok), GROUP * tok)
            out = dot_nn(big_ref[span, :], back).astype(BF)
            for q in range(GROUP):
                cols = pl.ds(pl.multiple_of((i * GROUP + q) * BLK, BLK), BLK)
                acc_ref[:, cols] = out[q * tok : (q + 1) * tok]
            return carry

        lax.fori_loop(0, blocks // GROUP, block, 0)

    for j in range(N_X):

        @pl.when(k == j)
        def _(j=j):
            out_ref[...] = acc_ref[:, pl.ds(j * seg, seg)]


def combine(x, tab, back):
    tok, total = tab.shape
    _, packed, _ = back.shape
    width = packed // CAP * BLK * N_C
    seg = width // (N_X * N_C)
    return pl.pallas_call(
        combine_kernel,
        grid_spec=pltpu.PrefetchScalarGridSpec(
            num_scalar_prefetch=1,
            grid=(N_C, N_X),
            in_specs=[
                pl.BlockSpec((tok, total), lambda c, k, x: (0, 0)),
                pl.BlockSpec((N_Z, 1, packed, BLK), lambda c, k, x: (0, c, 0, 0)),
            ],
            out_specs=pl.BlockSpec(
                (tok, seg), lambda c, k, x: (0, lax.bitwise_xor(x[0], k) * N_C + c)
            ),
            scratch_shapes=[
                pltpu.VMEM((packed // CAP * tok, total), BF),
                pltpu.VMEM((tok, width // N_C), BF),
            ],
        ),
        out_shape=like(tok, width),
        compiler_params=params(SHARE),
        cost_estimate=cost(COST),
        name="combine_rows",
    )(x, tab, back.reshape(N_Z, N_C, packed, BLK))


def gather_x(piece, near):
    far_side = near ^ 2
    got = {near: swap(piece, "x", near), far_side: swap(piece, "x", far_side)}
    return [piece, got[1], swap(got[far_side], "x", near), got[3]]


def scatter_x(here, pair, other, near):
    moved = swap(pair, "x", near)
    joint = (other.astype(F32) + moved[1].astype(F32)).astype(BF)
    return here, moved, swap(joint, "x", near ^ 2)


def gather_y(rows, step):
    ahead, behind = shift(rows, "y", -1), shift(rows, "y", 1)
    far = shift(behind if step == 1 else ahead, "y", step)
    return [rows, ahead, far, behind]


def scatter_y(pieces):
    return [pieces[0]] + [shift(pieces[k], "y", k) for k in (2, 1, 3)]


ANY = pl.BlockSpec(memory_space=pl.ANY)


def stacked(rows):
    return jnp.concatenate([r[...] for r in rows], axis=0)


def fetch(weights, lo, hi, buf, sem):
    k = pl.program_id(0)

    @pl.when(k == 0)
    def _():
        for j, w in enumerate(weights):
            pltpu.make_async_copy(
                w.at[:, pl.ds(lo, hi - lo)], buf.at[j], sem.at[j]
            ).start()

    for s in range(2):
        j = 2 * k + s
        pltpu.make_async_copy(
            weights[0].at[:, pl.ds(lo, hi - lo)], buf.at[j], sem.at[j]
        ).wait()
    return jnp.concatenate([buf[2 * k], buf[2 * k + 1]], axis=1)


def fetch_scratch(weights, lo, hi):
    count = len(weights)
    return [
        pltpu.VMEM((count, weights[0].shape[0], hi - lo), BF),
        pltpu.SemaphoreType.DMA((count,)),
    ]


def row_specs(count, chunk, seg):
    return [pl.BlockSpec((chunk, seg), lambda k: (0, k))] * count


def whole(shape):
    return pl.BlockSpec(shape, lambda k: (0,) * len(shape))


def project_kernel(lo, hi, *refs):
    rows, weights, (out_ref, buf, sem) = refs[:N_Y], refs[N_Y:-3], refs[-3:]
    part = dot_nn(stacked(rows), fetch(weights, lo, hi, buf, sem))

    @pl.when(pl.program_id(0) == 0)
    def _():
        out_ref[...] = part

    @pl.when(pl.program_id(0) > 0)
    def _():
        out_ref[...] += part


def project(rows, weights, lo, hi):
    chunk = rows[0].shape[0]
    seg = weights[0].shape[0]
    shape = (chunk * N_Y, 2 * (hi - lo))
    return pl.pallas_call(
        functools.partial(project_kernel, lo, hi),
        grid=(N_X,),
        in_specs=row_specs(N_Y, chunk, seg) + [ANY] * len(weights),
        out_specs=whole(shape),
        out_shape=like(*shape, dtype=F32),
        scratch_shapes=fetch_scratch(weights, lo, hi),
        compiler_params=params(SHARE),
        cost_estimate=cost(COST),
        name="project_rows",
    )(*rows, *weights)


def sum_cores(half, other):
    mid = half.shape[1] // 2
    return half[...] + jnp.concatenate([other[:, mid:], other[:, :mid]], axis=1)


def gates(pre, hid):
    for s in range(2):
        gate = pre[:, 2 * s * hid : (2 * s + 1) * hid]
        yield gate, pre[:, (2 * s + 1) * hid : (2 * s + 2) * hid], jax.nn.sigmoid(gate)


def spread_back(value_ref, weights, outs):
    part = lax.dot_general(
        value_ref[...], weights, (((1,), (1,)), ((), ())), preferred_element_type=F32
    ).astype(BF)
    chunk = part.shape[0] // N_Y
    for i, ref in enumerate(outs):
        ref[...] = part[i * chunk : (i + 1) * chunk]


def forward_kernel(lo, hi, half_ref, other_ref, *refs):
    weights, hidden_ref, outs, (buf, sem) = refs[:-7], refs[-7], refs[-6:-2], refs[-2:]

    @pl.when(pl.program_id(0) == 0)
    def _():
        pre = sum_cores(half_ref, other_ref)
        parts = [gate * sig * up for gate, up, sig in gates(pre, pre.shape[1] // 4)]
        hidden_ref[...] = jnp.concatenate(parts, axis=1).astype(BF)

    spread_back(hidden_ref, fetch(weights, lo, hi, buf, sem), outs)


def backward_kernel(lo, hi, half_ref, other_ref, ghalf_ref, gother_ref, *refs):
    weights, grad_ref, outs, (buf, sem) = refs[:-7], refs[-7], refs[-6:-2], refs[-2:]

    @pl.when(pl.program_id(0) == 0)
    def _():
        pre = sum_cores(half_ref, other_ref)
        hid = pre.shape[1] // 4
        grad_hidden = sum_cores(ghalf_ref, gother_ref)
        parts = []
        for s, (gate, up, sig) in enumerate(gates(pre, hid)):
            grad = grad_hidden[:, s * hid : (s + 1) * hid]
            parts += [grad * up * sig * (1.0 + gate * (1.0 - sig)), grad * (gate * sig)]
        grad_ref[...] = jnp.concatenate(parts, axis=1).astype(BF)

    spread_back(grad_ref, fetch(weights, lo, hi, buf, sem), outs)


def middle(kernel, name, halves, weights, lo, hi):
    count = halves[0].shape[0]
    seg = weights[0].shape[0]
    chunk = count // N_Y
    cols = 2 * (hi - lo)
    first, *pieces = pl.pallas_call(
        functools.partial(kernel, lo, hi),
        grid=(N_X,),
        in_specs=[whole(h.shape) for h in halves] + [ANY] * len(weights),
        out_specs=[whole((count, cols))]
        + row_specs(N_Y, chunk, seg),
        out_shape=[like(count, cols)] + [like(chunk, N_X * seg)] * N_Y,
        scratch_shapes=fetch_scratch(weights, lo, hi),
        compiler_params=params(SHARE),
        cost_estimate=cost(COST),
        name=name,
    )(*halves, *weights)
    return first, pieces


def weight_grad_kernel(hidden_ref, grad_ref, *refs):
    tok, cot, outs = refs[:N_Y], refs[N_Y : 2 * N_Y], refs[2 * N_Y : -2]
    buf, sem = refs[-2:]
    k = pl.program_id(0)
    hid = hidden_ref.shape[1] // 2
    dims = (((0,), (0,)), ((), ()))
    gate_up = lax.dot_general(stacked(tok), grad_ref[...], dims, preferred_element_type=F32)
    down = lax.dot_general(stacked(cot), hidden_ref[...], dims, preferred_element_type=F32)
    for s in range(2):
        buf[2 * k + s, :, : 2 * hid] = gate_up[:, 2 * s * hid : (2 * s + 2) * hid].astype(BF)
        buf[2 * k + s, :, 2 * hid :] = down[:, s * hid : (s + 1) * hid].astype(BF)
    def copies(j):
        for i, near in enumerate((1, 3)):
            here, pair, other = outs[3 * i : 3 * i + 3]
            dst = {0: here, near: pair.at[0], 2: pair.at[1], near ^ 2: other}[j]
            yield pltpu.make_async_copy(buf.at[2 * j + i], dst, sem.at[2 * j + i])

    for j in range(N_X):

        @pl.when(k == j)
        def _(j=j):
            for c in copies(j):
                c.start()

    @pl.when(k == N_X - 1)
    def _():
        for j in range(N_X):
            for c in copies(j):
                c.wait()


def weight_grad(hidden, grad_pre, tok_rows, cot_rows):
    hid = hidden.shape[1] // 2
    chunk, width = tok_rows[0].shape
    seg = width // N_X
    one, two = like(seg, 3 * hid), like(2, seg, 3 * hid)
    outs = [one, two, one, one, two, one]
    return pl.pallas_call(
        weight_grad_kernel,
        grid=(N_X,),
        in_specs=[whole(hidden.shape), whole(grad_pre.shape)]
        + row_specs(2 * N_Y, chunk, seg),
        out_specs=[ANY] * len(outs),
        out_shape=outs,
        scratch_shapes=[
            pltpu.VMEM((2 * N_X, seg, 3 * hid), BF),
            pltpu.SemaphoreType.DMA((2 * N_X,)),
        ],
        compiler_params=params(SHARE),
        cost_estimate=cost(COST),
        name="weight_grad",
    )(hidden, grad_pre, *tok_rows, *cot_rows)


def split_kernel(c_ref, keep_in, give_in, keep_ref, give_ref):
    del c_ref
    keep_ref[...] = keep_in[0].astype(BF)
    give_ref[...] = give_in[0].astype(BF)


def split_master(c, master):
    _, quarter, cols = master.shape
    seg = quarter // N_C
    out = like(seg, cols)
    return pl.pallas_call(
        split_kernel,
        grid_spec=pltpu.PrefetchScalarGridSpec(
            num_scalar_prefetch=1,
            grid=(1,),
            in_specs=[
                pl.BlockSpec((1, seg, cols), lambda i, c: (0, c[0], 0)),
                pl.BlockSpec((1, seg, cols), lambda i, c: (0, 1 - c[0], 0)),
            ],
            out_specs=[pl.BlockSpec((seg, cols), lambda i, c: (0, 0))] * 2,
        ),
        out_shape=[out, out],
        compiler_params=params(ROOM),
        cost_estimate=cost(COST),
        name="split_master",
    )(c, master, master)


def update_kernel(c_ref, master_ref, sums_ref, other_ref, *refs):
    *parts, new_ref, out_ref, grad_ref = refs
    here = pl.program_id(0) == c_ref[0]

    @pl.when(here)
    def _():
        grad_ref[...] = sum(p[...].astype(F32) for p in parts).astype(BF).astype(F32)

    @pl.when(jnp.logical_not(here))
    def _():
        grad_ref[...] = other_ref[...].astype(F32)

    seg, cols = grad_ref.shape
    hid = cols // 3
    ones = jnp.ones((8, hid), F32)
    means = []
    for g in range(3):
        grad = grad_ref[:, g * hid : (g + 1) * hid]
        total = lax.dot_general(
            ones,
            grad * grad,
            (((1,), (1,)), ((), ())),
            precision=lax.Precision.HIGHEST,
            preferred_element_type=F32,
        )
        means.append(total[:1] / hid)
    sums = sums_ref[0] + jnp.concatenate(means, axis=0)
    out_ref[0] = sums
    scale = LEARN_RATE / (jnp.sqrt(sums) + EPSILON)
    tall = jnp.concatenate([scale, jnp.zeros((125, seg), F32)], axis=0).T
    for g in range(3):
        span = pl.ds(g * hid, hid)
        new_ref[:, span] = (master_ref[0, :, span] - grad_ref[:, span] * tall[:, g : g + 1]).astype(BF)


def update(c, master, sums, other, *parts):
    _, quarter, cols = master.shape
    seg = quarter // N_C
    piece = pl.BlockSpec((seg, cols), lambda h, c: (0, 0))
    first = pl.BlockSpec((pl.squeezed, seg, cols), lambda h, c: (0, 0, 0))
    rows = pl.BlockSpec((seg, cols), lambda h, c: (h, 0))
    lanes = pl.BlockSpec((1, 3, seg), lambda h, c: (0, 0, h))
    return pl.pallas_call(
        update_kernel,
        grid_spec=pltpu.PrefetchScalarGridSpec(
            num_scalar_prefetch=1,
            grid=(N_C,),
            in_specs=[pl.BlockSpec((1, seg, cols), lambda h, c: (0, h, 0)), lanes]
            + [piece, piece, first, piece],
            out_specs=[rows, lanes],
            scratch_shapes=[pltpu.VMEM((seg, cols), F32)],
        ),
        out_shape=[like(quarter, cols), like(*sums.shape, dtype=F32)],
        compiler_params=params(SHARE),
        cost_estimate=cost(COST),
        name="update_master",
    )(c, master, sums, other, *parts)


def copy_kernel(in_ref, out_ref):
    out_ref[0] = in_ref[...]


def placed(rows):
    count, cols = rows.shape
    return pl.pallas_call(
        copy_kernel,
        grid=(2,),
        in_specs=[pl.BlockSpec((count // 2, cols), lambda i: (i, 0))],
        out_specs=pl.BlockSpec((1, count // 2, cols), lambda i: (0, i, 0)),
        out_shape=like(1, count, cols),
        compiler_params=params(SHARE),
        cost_estimate=cost(COST),
        name="place_weights",
    )(rows)


def exchange(blocks):
    return lax.all_to_all(blocks, ("z", "c"), split_axis=0, concat_axis=0, tiled=True)


def local(tokens, cotangent, route_ids, router_weights, master, accumulator):
    hid = master.shape[2] // 3
    x = lax.axis_index("x").reshape(1)
    core = lax.axis_index("c").reshape(1)
    merge = lambda a: a.reshape((N_Z * N_C,) + a.shape[2:])

    tok_send, out_tab, in_tab = select(x, route_ids, router_weights, tokens, False, True)
    tok_packed = exchange(merge(tok_send))
    (cot_send,) = select(x, route_ids, router_weights, after(cotangent, tok_send), True, False)
    cot_packed = exchange(merge(cot_send))

    own, give = split_master(core, master)
    got = swap_core(give)
    own_weights = gather_x(own, 1)
    got_weights = gather_x(got, 3)
    weights = [w for pair in zip(own_weights, got_weights) for w in pair]

    tok_packed = after(tok_packed, own_weights[1], own_weights[3])
    tok_rows = gather_y(unpack(tok_packed), 1)
    cot_packed = after(cot_packed, tok_rows[1], tok_rows[3], got_weights[1], got_weights[3])
    cot_rows = gather_y(unpack(cot_packed), -1)

    pre = project(tok_rows, weights, 0, 2 * hid)
    pre_other = swap_core(pre)
    hidden, out_pieces = middle(
        forward_kernel, "forward_rows", (pre, pre_other), weights, 2 * hid, 3 * hid
    )
    grad_hidden = project(cot_rows, weights, 2 * hid, 3 * hid)
    grad_other = after(swap_core(grad_hidden), hidden)
    grad_pre, in_pieces = middle(
        backward_kernel,
        "backward_rows",
        (pre, pre_other, grad_hidden, grad_other),
        weights,
        0,
        2 * hid,
    )
    grads = weight_grad(hidden, grad_pre, tok_rows, cot_rows)

    out_parts = scatter_y(out_pieces)
    in_pieces = [after(p, *grads[1::3]) for p in in_pieces]
    in_parts = scatter_y(in_pieces)
    own_parts = scatter_x(*grads[:3], 1)
    here, moved, joint = scatter_x(*grads[3:], 3)

    out_back = exchange(pack(*out_parts))
    in_back = exchange(pack(*in_parts))

    output = combine(x, out_tab, out_back)
    joint = after(joint, out_back)
    got_grad = sum(p.astype(F32) for p in (here, moved[0], joint)).astype(BF)
    new, sums = update(core, master, accumulator, swap_core(got_grad), *own_parts)
    new_weights = placed(swap_core(new))

    input_grad = combine(x, in_tab, in_back)
    return output, input_grad, new_weights, sums


def solution(mesh):
    fine = Mesh(mesh.devices.reshape(N_X, N_Z, N_Y, N_C), ("x", "z", "y", "c"))
    rows = P(("x", "z", "y", "c"), None)
    weights = P(("z", "y", "c"), "x", None)
    sums = P(("z", "y", "c"), None, "x")
    return jax.shard_map(
        local,
        mesh=fine,
        in_specs=(rows, rows, rows, rows, weights, sums),
        out_specs=(rows, rows, weights, sums),
        check_vma=False,
    )
```

profile of v0, /device:TPU:1, one launch (start us, length us, event | category | flops | bytes accessed | tf_op | source)
XLA Modules:
  0.0 195.2 jit_solution(9735089550663203432)
XLA Ops:
  0.7 3.0 %split_master.1 = (bf16[896,384]{1,0:T(8,128)(2,1)}, bf16[896,384]{1,0:T(8,128)(2,1)}) custom-call(s32[1]{0:T(128)} %bitcast.2.c_ref, f32[1,1792,384]{2,1,0:T(8,128)} %master_ref.1, f32[1,1792,384]{2,1,0:T(8,128)} %master_ref.1), custom_call_target="tpu_custom_call" | custom-call | flops 99999997952 | bytes 100000000 | tf_op jit(solution)/shard_map/split_master/pallas_call | solution.py:522
  7.8 3.5 %select_tok.1 = (bf16[8,2,72,256]{3,2,1,0:T(8,128)(2,1)}, bf16[128,576]{1,0:T(8,128)(2,1)S(1)}, bf16[128,576]{1,0:T(8,128)(2,1)S(1)}) custom-call(s32[1]{0:T(128)} %bitcast.x_ref, s32[128,8]{1,0:T(8,128)S(1)} %copy.10.ids_ref, f32[128,8]{1,0:T(8,128)S(1)} %copy.11.w_ref, bf16[128,7168]{1,0:T(8,128)(2,1)S(1)} %copy-done.1, bf16[128,7168]{1,0:T(8,128)(2,1)S(1)} %copy-done.1, ...), custom_call_target="tpu_custom_call" | custom-call | flops 99999997952 | bytes 100000000 | tf_op jit(solution)/shard_map/select_tok/pallas_call | solution.py:144
  11.3 9.7 %all-to-all-start = ((bf16[16,72,256]{2,1,0:T(8,128)(2,1)}), bf16[16,72,256]{2,1,0:T(8,128)(2,1)S(1)}, u32[]{:S(2)}, u32[]{:S(2)}) async-start(bf16[16,72,256]{2,1,0:T(8,128)(2,1)} %bitcast.1), calls=%async_computation | async-start | bytes 1179648 | tf_op jit(solution)/shard_map/all_to_all | solution.py:618
  22.7 3.4 %select_cot.1 = bf16[8,2,72,256]{3,2,1,0:T(8,128)(2,1)} custom-call(s32[1]{0:T(128)} %bitcast.x_ref, s32[128,8]{1,0:T(8,128)S(1)} %copy.10.ids_ref, f32[128,8]{1,0:T(8,128)S(1)} %copy.11.w_ref, bf16[128,7168]{1,0:T(8,128)(2,1)S(1)} %copy-done.2, bf16[128,7168]{1,0:T(8,128)(2,1)S(1)} %copy-done.2, bf16[128,7168]{1,0:T(8,128)(2,1)S(1)} %copy-done.2, ...), custom_call_target="tpu_custom_call" | custom-call | flops 99999997952 | bytes 100000000 | tf_op jit(solution)/shard_map/select_cot/pallas_call | solution.py:144
  27.0 12.6 %all-to-all-done.in_ref = bf16[16,72,256]{2,1,0:T(8,128)(2,1)S(1)} async-done(((bf16[16,72,256]{2,1,0:T(8,128)(2,1)}), bf16[16,72,256]{2,1,0:T(8,128)(2,1)S(1)}, u32[]{:S(2)}, u32[]{:S(2)}) %all-to-all-start) | async-done | bytes 589856 | tf_op jit(solution)/shard_map/all_to_all | solution.py:618
  39.6 3.5 %all-to-all-start.2 = ((bf16[16,72,256]{2,1,0:T(8,128)(2,1)}), bf16[16,72,256]{2,1,0:T(8,128)(2,1)S(1)}, u32[]{:S(2)}, u32[]{:S(2)}) async-start(bf16[16,72,256]{2,1,0:T(8,128)(2,1)} %bitcast.4), calls=%async_computation.2 | async-start | bytes 1179648 | tf_op jit(solution)/shard_map/all_to_all | solution.py:618
  49.0 12.3 %all-to-all-done.2.in_ref = bf16[16,72,256]{2,1,0:T(8,128)(2,1)S(1)} async-done(((bf16[16,72,256]{2,1,0:T(8,128)(2,1)}), bf16[16,72,256]{2,1,0:T(8,128)(2,1)S(1)}, u32[]{:S(2)}, u32[]{:S(2)}) %all-to-all-start.2) | async-done | bytes 589856 | tf_op jit(solution)/shard_map/all_to_all | solution.py:618
  61.3 2.9 %collective-permute-done.3.refs_3_ = bf16[80,3584]{1,0:T(8,128)(2,1)} collective-permute-done((bf16[80,3584]{1,0:T(8,128)(2,1)}, bf16[80,3584]{1,0:T(8,128)(2,1)}, u32[]{:S(2)}, u32[]{:S(2)}) %collective-permute-start.3) | collective-permute-done | bytes 573472 | tf_op jit(solution)/shard_map/ppermute | solution.py:33
  67.4 12.0 %collective-permute-done.14.refs_1_.refs_5_ = bf16[80,3584]{1,0:T(8,128)(2,1)S(1)} collective-permute-done((bf16[80,3584]{1,0:T(8,128)(2,1)S(1)}, bf16[80,3584]{1,0:T(8,128)(2,1)S(1)}, u32[]{:S(2)}, u32[]{:S(2)}) %collective-permute-start.14) | collective-permute-done | bytes 573472 | tf_op jit(solution)/shard_map/ppermute | solution.py:33
  81.3 4.7 %project_rows.2.half_ref = f32[320,512]{1,0:T(8,128)S(1)} custom-call(bf16[80,3584]{1,0:T(8,128)(2,1)} %unpack_rows.2.refs_0_, bf16[80,3584]{1,0:T(8,128)(2,1)} %collective-permute-done.2.refs_1_, bf16[80,3584]{1,0:T(8,128)(2,1)S(1)} %collective-permute-done.4.refs_2_, bf16[80,3584]{1,0:T(8,128)(2,1)} %collective-permute-done.3.refs_3_, ...), custom_call_target="tpu_custom_call" | custom-call | flops 99999997952 | bytes 100000000 | tf_op jit(solution)/shard_map/project_rows/pallas_call | solution.py:376
  88.8 4.7 %collective-permute-done.16.refs_3_.refs_7_ = bf16[80,3584]{1,0:T(8,128)(2,1)S(1)} collective-permute-done((bf16[80,3584]{1,0:T(8,128)(2,1)S(1)}, bf16[80,3584]{1,0:T(8,128)(2,1)S(1)}, u32[]{:S(2)}, u32[]{:S(2)}) %collective-permute-start.16) | collective-permute-done | bytes 573472 | tf_op jit(solution)/shard_map/ppermute | solution.py:33
  97.9 3.5 %forward_rows.1 = (bf16[320,256]{1,0:T(8,128)(2,1)S(1)}, bf16[80,3584]{1,0:T(8,128)(2,1)S(1)}, bf16[80,3584]{1,0:T(8,128)(2,1)}, bf16[80,3584]{1,0:T(8,128)(2,1)}, bf16[80,3584]{1,0:T(8,128)(2,1)}) custom-call(f32[320,512]{1,0:T(8,128)S(1)} %project_rows.2.half_ref, f32[320,512]{1,0:T(8,128)S(1)} %collective-permute-done.10.other_ref, ...), custom_call_target="tpu_custom_call" | custom-call | flops 99999997952 | bytes 100000000 | tf_op jit(solution)/shard_map/forward_rows/pallas_call | solution.py:443
  105.4 4.2 %backward_rows.1 = (bf16[320,512]{1,0:T(8,128)(2,1)S(1)}, bf16[80,3584]{1,0:T(8,128)(2,1)S(1)}, bf16[80,3584]{1,0:T(8,128)(2,1)}, bf16[80,3584]{1,0:T(8,128)(2,1)}, bf16[80,3584]{1,0:T(8,128)(2,1)}) custom-call(f32[320,512]{1,0:T(8,128)S(1)} %project_rows.2.half_ref, f32[320,512]{1,0:T(8,128)S(1)} %collective-permute-done.10.other_ref, ...), custom_call_target="tpu_custom_call" | custom-call | flops 99999997952 | bytes 100000000 | tf_op jit(solution)/shard_map/backward_rows/pallas_call | solution.py:443
  109.6 7.2 %weight_grad.1 = (bf16[896,384]{1,0:T(8,128)(2,1)S(1)}, bf16[2,896,384]{2,1,0:T(8,128)(2,1)}, bf16[896,384]{1,0:T(8,128)(2,1)S(1)}, bf16[896,384]{1,0:T(8,128)(2...) custom-call(bf16[320,256]{1,0:T(8,128)(2,1)S(1)} %get-tuple-element.48.hidden_ref, ...), custom_call_target="tpu_custom_call" | custom-call | flops 99999997952 | bytes 100000000 | tf_op jit(solution)/shard_map/weight_grad/pallas_call | solution.py:495
  119.8 11.0 %collective-permute-done.12.refs_2_ = bf16[80,3584]{1,0:T(8,128)(2,1)} collective-permute-done((bf16[80,3584]{1,0:T(8,128)(2,1)}, bf16[80,3584]{1,0:T(8,128)(2,1)}, u32[]{:S(2)}, u32[]{:S(2)}) %collective-permute-start.12) | collective-permute-done | bytes 573472 | tf_op jit(solution)/shard_map/ppermute | solution.py:33
  133.5 3.5 %pack_rows.2 = bf16[16,72,256]{2,1,0:T(8,128)(2,1)} custom-call(bf16[80,3584]{1,0:T(8,128)(2,1)S(1)} %get-tuple-element.41.refs_0_, bf16[80,3584]{1,0:T(8,128)(2,1)} %collective-permute-done.11.refs_1_, bf16[80,3584]{1,0:T(8,128)(2,1)} %collective-permute-done.12.refs_2_, bf16[80,3584]{1,0:T(8,128)(2,1)} %collective-permute-done.13.refs_3_), custom_call_target="tpu_custom_call" | custom-call | flops 99999997952 | bytes 100000000 | tf_op jit(solution)/shard_map/pack_rows/pallas_call | solution.py:217
  137.1 6.7 %all-to-all-start.1 = ((bf16[16,72,256]{2,1,0:T(8,128)(2,1)}), bf16[16,72,256]{2,1,0:T(8,128)(2,1)S(1)}, u32[]{:S(2)}, u32[]{:S(2)}) async-start(bf16[16,72,256]{2,1,0:T(8,128)(2,1)} %pack_rows.2), calls=%async_computation.1 | async-start | bytes 1179648 | tf_op jit(solution)/shard_map/all_to_all | solution.py:618
  143.8 6.3 %collective-permute-done.21 = bf16[2,896,384]{2,1,0:T(8,128)(2,1)} collective-permute-done((bf16[2,896,384]{2,1,0:T(8,128)(2,1)}, bf16[2,896,384]{2,1,0:T(8,128)(2,1)}, u32[]{:S(2)}, u32[]{:S(2)}) %collective-permute-start.21) | collective-permute-done | bytes 1376288 | tf_op jit(solution)/shard_map/ppermute | solution.py:28
  152.2 2.9 %collective-permute-done.19.refs_2_ = bf16[80,3584]{1,0:T(8,128)(2,1)} collective-permute-done((bf16[80,3584]{1,0:T(8,128)(2,1)}, bf16[80,3584]{1,0:T(8,128)(2,1)}, u32[]{:S(2)}, u32[]{:S(2)}) %collective-permute-start.19) | collective-permute-done | bytes 573472 | tf_op jit(solution)/shard_map/ppermute | solution.py:33
  155.1 3.5 %pack_rows.3 = bf16[16,72,256]{2,1,0:T(8,128)(2,1)} custom-call(bf16[80,3584]{1,0:T(8,128)(2,1)S(1)} %copy-done.17, bf16[80,3584]{1,0:T(8,128)(2,1)S(1)} %collective-permute-done.18.refs_1_, bf16[80,3584]{1,0:T(8,128)(2,1)} %collective-permute-done.19.refs_2_, bf16[80,3584]{1,0:T(8,128)(2,1)} %collective-permute-done.20.refs_3_), custom_call_target="tpu_custom_call" | custom-call | flops 99999997952 | bytes 100000000 | tf_op jit(solution)/shard_map/pack_rows/pallas_call | solution.py:217
  162.4 5.5 %all-to-all-start.3 = ((bf16[16,72,256]{2,1,0:T(8,128)(2,1)}), bf16[16,72,256]{2,1,0:T(8,128)(2,1)}, u32[]{:S(2)}, u32[]{:S(2)}) async-start(bf16[16,72,256]{2,1,0:T(8,128)(2,1)} %pack_rows.3), calls=%async_computation.3 | async-start | bytes 1179648 | tf_op jit(solution)/shard_map/all_to_all | solution.py:618
  171.7 5.4 %combine_rows.2 = bf16[128,7168]{1,0:T(8,128)(2,1)} custom-call(s32[1]{0:T(128)} %bitcast.x_ref, bf16[128,576]{1,0:T(8,128)(2,1)S(1)} %copy-done.19, bf16[8,2,72,256]{3,2,1,0:T(8,128)(2,1)S(1)} %bitcast.21), custom_call_target="tpu_custom_call" | custom-call | flops 99999997952 | bytes 100000000 | tf_op jit(solution)/shard_map/combine_rows/pallas_call | solution.py:272
  178.4 5.3 %update_master.1 = (bf16[1792,384]{1,0:T(8,128)(2,1)S(1)}, f32[1,3,1792]{2,1,0:T(4,128)S(1)}) custom-call(s32[1]{0:T(128)} %bitcast.2.c_ref, f32[1,1792,384]{2,1,0:T(8,128)S(1)} %copy-done, f32[1,3,1792]{2,1,0:T(4,128)S(1)} %copy.14.sums_ref, bf16[896,384]{1,0:T(8,128)(2,1)S(1)} %collective-permute-done.23.other_ref, bf16[896,384]{1,0:T(8,128)(2,1)S(1)} %copy-done.15, ...), custom_call_target="tpu_custom_call" | custom-call | flops 99999997952 | bytes 100000000 | tf_op jit(solution)/shard_map/update_master/pallas_call | solution.py:582
  186.7 6.8 %combine_rows.3 = bf16[128,7168]{1,0:T(8,128)(2,1)} custom-call(s32[1]{0:T(128)} %bitcast.x_ref, bf16[128,576]{1,0:T(8,128)(2,1)S(1)} %get-tuple-element.45.tab_ref, bf16[8,2,72,256]{3,2,1,0:T(8,128)(2,1)} %bitcast.5.back_ref), custom_call_target="tpu_custom_call" | custom-call | flops 99999997952 | bytes 100000000 | tf_op jit(solution)/shard_map/combine_rows/pallas_call | solution.py:272
  (109 shorter events, 49.9 us)
Async XLA Ops:
  3.7 39.4 %collective-permute-start = (bf16[896,384]{1,0:T(8,128)(2,1)}, bf16[896,384]{1,0:T(8,128)(2,1)}, u32[]{:S(2)}, u32[]{:S(2)}) collective-permute-start(bf16[896,384]{1,0:T(8,128)(2,1)} %get-tuple-element.38.refs_4_.refs_0_), channel_id=1, source_target_pairs={{0,64},{64,0},{128,192},{192,128},{1,65},{65,1},{129,193},{193,129... | collective-permute-start | bytes 2064392 | tf_op jit(solution)/shard_map/ppermute | solution.py:28
  5.7 37.4 %collective-permute-start.1 = (bf16[896,384]{1,0:T(8,128)(2,1)}, bf16[896,384]{1,0:T(8,128)(2,1)}, u32[]{:S(2)}, u32[]{:S(2)}) collective-permute-start(bf16[896,384]{1,0:T(8,128)(2,1)} %get-tuple-element.38.refs_4_.refs_0_), channel_id=1, source_target_pairs={{0,192},{64,128},{128,64},{192,0},{1,193},{65,129},{129,65},{193,1... | collective-permute-start | bytes 2064392 | tf_op jit(solution)/shard_map/ppermute | solution.py:28
  11.3 28.4 %all-to-all-start = ((bf16[16,72,256]{2,1,0:T(8,128)(2,1)}), bf16[16,72,256]{2,1,0:T(8,128)(2,1)S(1)}, u32[]{:S(2)}, u32[]{:S(2)}) async-start(bf16[16,72,256]{2,1,0:T(8,128)(2,1)} %bitcast.1), calls=%async_computation | async-start | bytes 1179648 | tf_op jit(solution)/shard_map/all_to_all | solution.py:618
  26.1 22.3 %collective-permute-start.6 = (bf16[896,384]{1,0:T(8,128)(2,1)S(1)}, bf16[896,384]{1,0:T(8,128)(2,1)S(1)}, u32[]{:S(2)}, u32[]{:S(2)}) collective-permute-start(bf16[896,384]{1,0:T(8,128)(2,1)S(1)} %collective-permute-done.5.refs_5_.refs_1_), channel_id=1, source_target_pairs={{0,64},{64,0},{128,192},{192,128},{1,65},{65,1},{129,193},{193,129... | collective-permute-start | bytes 2064392 | tf_op jit(solution)/shard_map/ppermute | solution.py:28
  26.4 34.9 %collective-permute-start.9 = (bf16[896,384]{1,0:T(8,128)(2,1)S(1)}, bf16[896,384]{1,0:T(8,128)(2,1)S(1)}, u32[]{:S(2)}, u32[]{:S(2)}) collective-permute-start(bf16[896,384]{1,0:T(8,128)(2,1)S(1)} %collective-permute-done.5.refs_5_.refs_1_), channel_id=1, source_target_pairs={{0,192},{64,128},{128,64},{192,0},{1,193},{65,129},{129,65},{193,1... | collective-permute-start | bytes 2064392 | tf_op jit(solution)/shard_map/ppermute | solution.py:28
  39.6 21.6 %all-to-all-start.2 = ((bf16[16,72,256]{2,1,0:T(8,128)(2,1)}), bf16[16,72,256]{2,1,0:T(8,128)(2,1)S(1)}, u32[]{:S(2)}, u32[]{:S(2)}) async-start(bf16[16,72,256]{2,1,0:T(8,128)(2,1)} %bitcast.4), calls=%async_computation.2 | async-start | bytes 1179648 | tf_op jit(solution)/shard_map/all_to_all | solution.py:618
  45.3 16.0 %collective-permute-start.2 = (bf16[80,3584]{1,0:T(8,128)(2,1)}, bf16[80,3584]{1,0:T(8,128)(2,1)}, u32[]{:S(2)}, u32[]{:S(2)}) collective-permute-start(bf16[80,3584]{1,0:T(8,128)(2,1)} %unpack_rows.2.refs_0_), channel_id=1, source_target_pairs={{0,6},{2,0},{4,2},{6,4},{1,7},{3,1},{5,3},{7,5},{8,14},{10,8},{12,... | collective-permute-start | bytes 1720328 | tf_op jit(solution)/shard_map/ppermute | solution.py:33
  48.0 16.2 %collective-permute-start.3 = (bf16[80,3584]{1,0:T(8,128)(2,1)}, bf16[80,3584]{1,0:T(8,128)(2,1)}, u32[]{:S(2)}, u32[]{:S(2)}) collective-permute-start(bf16[80,3584]{1,0:T(8,128)(2,1)} %unpack_rows.2.refs_0_), channel_id=1, source_target_pairs={{0,2},{2,4},{4,6},{6,0},{1,3},{3,5},{5,7},{7,1},{8,10},{10,12},{12... | collective-permute-start | bytes 1720328 | tf_op jit(solution)/shard_map/ppermute | solution.py:33
  48.0 33.3 %collective-permute-start.7 = (bf16[896,384]{1,0:T(8,128)(2,1)}, bf16[896,384]{1,0:T(8,128)(2,1)}, u32[]{:S(2)}, u32[]{:S(2)}) collective-permute-start(bf16[896,384]{1,0:T(8,128)(2,1)} %collective-permute-done.1.refs_10_.refs_6_), channel_id=1, source_target_pairs={{0,64},{64,0},{128,192},{192,128},{1,65},{65,1},{129,193},{193,129... | collective-permute-start | bytes 2064392 | tf_op jit(solution)/shard_map/ppermute | solution.py:28
  48.3 33.0 %collective-permute-start.8 = (bf16[896,384]{1,0:T(8,128)(2,1)S(1)}, bf16[896,384]{1,0:T(8,128)(2,1)}, u32[]{:S(2)}, u32[]{:S(2)}) collective-permute-start(bf16[896,384]{1,0:T(8,128)(2,1)S(1)} %collective-permute-done.6.refs_7_.refs_3_), channel_id=1, source_target_pairs={{0,192},{64,128},{128,64},{192,0},{1,193},{65,129},{129,65},{193,1... | collective-permute-start | bytes 2064392 | tf_op jit(solution)/shard_map/ppermute | solution.py:28
  66.0 15.3 %collective-permute-start.4 = (bf16[80,3584]{1,0:T(8,128)(2,1)}, bf16[80,3584]{1,0:T(8,128)(2,1)S(1)}, u32[]{:S(2)}, u32[]{:S(2)}) collective-permute-start(bf16[80,3584]{1,0:T(8,128)(2,1)} %collective-permute-done.3.refs_3_), channel_id=1, source_target_pairs={{0,2},{2,4},{4,6},{6,0},{1,3},{3,5},{5,7},{7,1},{8,10},{10,12},{12... | collective-permute-start | bytes 1720328 | tf_op jit(solution)/shard_map/ppermute | solution.py:33
  67.2 26.3 %collective-permute-start.16 = (bf16[80,3584]{1,0:T(8,128)(2,1)S(1)}, bf16[80,3584]{1,0:T(8,128)(2,1)S(1)}, u32[]{:S(2)}, u32[]{:S(2)}) collective-permute-start(bf16[80,3584]{1,0:T(8,128)(2,1)S(1)} %unpack_rows.3.refs_0_.refs_4_), channel_id=1, source_target_pairs={{0,2},{2,4},{4,6},{6,0},{1,3},{3,5},{5,7},{7,1},{8,10},{10,12},{12... | collective-permute-start | bytes 1720328 | tf_op jit(solution)/shard_map/ppermute | solution.py:33
  101.4 17.3 %collective-permute-start.11 = (bf16[80,3584]{1,0:T(8,128)(2,1)}, bf16[80,3584]{1,0:T(8,128)(2,1)}, u32[]{:S(2)}, u32[]{:S(2)}) collective-permute-start(bf16[80,3584]{1,0:T(8,128)(2,1)} %get-tuple-element.42), channel_id=1, source_target_pairs={{0,4},{2,6},{4,0},{6,2},{1,5},{3,7},{5,1},{7,3},{8,12},{10,14},{12... | collective-permute-start | bytes 1720328 | tf_op jit(solution)/shard_map/ppermute | solution.py:33
  102.7 28.2 %collective-permute-start.12 = (bf16[80,3584]{1,0:T(8,128)(2,1)}, bf16[80,3584]{1,0:T(8,128)(2,1)}, u32[]{:S(2)}, u32[]{:S(2)}) collective-permute-start(bf16[80,3584]{1,0:T(8,128)(2,1)} %get-tuple-element.43), channel_id=1, source_target_pairs={{0,2},{2,4},{4,6},{6,0},{1,3},{3,5},{5,7},{7,1},{8,10},{10,12},{12... | collective-permute-start | bytes 1720328 | tf_op jit(solution)/shard_map/ppermute | solution.py:33
  104.7 26.1 %collective-permute-start.13 = (bf16[80,3584]{1,0:T(8,128)(2,1)}, bf16[80,3584]{1,0:T(8,128)(2,1)}, u32[]{:S(2)}, u32[]{:S(2)}) collective-permute-start(bf16[80,3584]{1,0:T(8,128)(2,1)} %get-tuple-element.44), channel_id=1, source_target_pairs={{0,6},{2,0},{4,2},{6,4},{1,7},{3,1},{5,3},{7,5},{8,14},{10,8},{12,... | collective-permute-start | bytes 1720328 | tf_op jit(solution)/shard_map/ppermute | solution.py:33
  117.7 32.3 %collective-permute-start.21 = (bf16[2,896,384]{2,1,0:T(8,128)(2,1)}, bf16[2,896,384]{2,1,0:T(8,128)(2,1)}, u32[]{:S(2)}, u32[]{:S(2)}) collective-permute-start(bf16[2,896,384]{2,1,0:T(8,128)(2,1)} %get-tuple-element.53), channel_id=1, source_target_pairs={{0,192},{64,128},{128,64},{192,0},{1,193},{65,129},{129,65},{193,1... | collective-permute-start | bytes 4128776 | tf_op jit(solution)/shard_map/ppermute | solution.py:28
  118.6 40.0 %collective-permute-start.24 = (bf16[2,896,384]{2,1,0:T(8,128)(2,1)}, bf16[2,896,384]{2,1,0:T(8,128)(2,1)}, u32[]{:S(2)}, u32[]{:S(2)}) collective-permute-start(bf16[2,896,384]{2,1,0:T(8,128)(2,1)} %get-tuple-element.52), channel_id=1, source_target_pairs={{0,64},{64,0},{128,192},{192,128},{1,65},{65,1},{129,193},{193,129... | collective-permute-start | bytes 4128776 | tf_op jit(solution)/shard_map/ppermute | solution.py:28
  118.6 33.6 %collective-permute-start.18 = (bf16[80,3584]{1,0:T(8,128)(2,1)}, bf16[80,3584]{1,0:T(8,128)(2,1)S(1)}, u32[]{:S(2)}, u32[]{:S(2)}) collective-permute-start(bf16[80,3584]{1,0:T(8,128)(2,1)} %get-tuple-element.56), channel_id=1, source_target_pairs={{0,4},{2,6},{4,0},{6,2},{1,5},{3,7},{5,1},{7,3},{8,12},{10,14},{12... | collective-permute-start | bytes 1720328 | tf_op jit(solution)/shard_map/ppermute | solution.py:33
  130.8 24.3 %collective-permute-start.19 = (bf16[80,3584]{1,0:T(8,128)(2,1)}, bf16[80,3584]{1,0:T(8,128)(2,1)}, u32[]{:S(2)}, u32[]{:S(2)}) collective-permute-start(bf16[80,3584]{1,0:T(8,128)(2,1)} %get-tuple-element.58), channel_id=1, source_target_pairs={{0,2},{2,4},{4,6},{6,0},{1,3},{3,5},{5,7},{7,1},{8,10},{10,12},{12... | collective-permute-start | bytes 1720328 | tf_op jit(solution)/shard_map/ppermute | solution.py:33
  130.8 24.3 %collective-permute-start.20 = (bf16[80,3584]{1,0:T(8,128)(2,1)}, bf16[80,3584]{1,0:T(8,128)(2,1)}, u32[]{:S(2)}, u32[]{:S(2)}) collective-permute-start(bf16[80,3584]{1,0:T(8,128)(2,1)} %get-tuple-element.60), channel_id=1, source_target_pairs={{0,6},{2,0},{4,2},{6,4},{1,7},{3,1},{5,3},{7,5},{8,14},{10,8},{12,... | collective-permute-start | bytes 1720328 | tf_op jit(solution)/shard_map/ppermute | solution.py:33
  137.1 25.4 %all-to-all-start.1 = ((bf16[16,72,256]{2,1,0:T(8,128)(2,1)}), bf16[16,72,256]{2,1,0:T(8,128)(2,1)S(1)}, u32[]{:S(2)}, u32[]{:S(2)}) async-start(bf16[16,72,256]{2,1,0:T(8,128)(2,1)} %pack_rows.2), calls=%async_computation.1 | async-start | bytes 1179648 | tf_op jit(solution)/shard_map/all_to_all | solution.py:618
  152.2 15.8 %collective-permute-start.22 = (bf16[896,384]{1,0:T(8,128)(2,1)}, bf16[896,384]{1,0:T(8,128)(2,1)S(1)}, u32[]{:S(2)}, u32[]{:S(2)}) collective-permute-start(bf16[896,384]{1,0:T(8,128)(2,1)} %fusion.1), channel_id=1, source_target_pairs={{0,64},{64,0},{128,192},{192,128},{1,65},{65,1},{129,193},{193,129... | collective-permute-start | bytes 2064392 | tf_op jit(solution)/shard_map/ppermute | solution.py:28
  160.7 17.7 %collective-permute-start.25 = (bf16[896,384]{1,0:T(8,128)(2,1)}, bf16[896,384]{1,0:T(8,128)(2,1)S(1)}, u32[]{:S(2)}, u32[]{:S(2)}) collective-permute-start(bf16[896,384]{1,0:T(8,128)(2,1)} %fusion), channel_id=1, source_target_pairs={{0,192},{64,128},{128,64},{192,0},{1,193},{65,129},{129,65},{193,1... | collective-permute-start | bytes 2064392 | tf_op jit(solution)/shard_map/ppermute | solution.py:28
  162.4 24.3 %all-to-all-start.3 = ((bf16[16,72,256]{2,1,0:T(8,128)(2,1)}), bf16[16,72,256]{2,1,0:T(8,128)(2,1)}, u32[]{:S(2)}, u32[]{:S(2)}) async-start(bf16[16,72,256]{2,1,0:T(8,128)(2,1)} %pack_rows.3), calls=%async_computation.3 | async-start | bytes 1179648 | tf_op jit(solution)/shard_map/all_to_all | solution.py:618
  (31 other events, 275.8 us)
where the time goes:
time: 196 us; the launch traced here: 195 us
  waiting for transfers between devices  68.2 us (35%)
  Pallas kernels  61.4 us (31%)
  starting transfers between devices  55.8 us (28%)
  other arithmetic  5.63 us (3%)
  local copies, waits for them, and re-layouts  3.27 us (2%)
    ppermute x12, waiting for transfers between devices, shift(): return lax.ppermute(a, axis, [(i, (i + step) % n) for i in range(n)])  33.6 us
    all_to_all x4, waiting for transfers between devices, exchange(): lax.all_to_all(blocks, ('z', 'c'), split_axis=0, concat_axis=0, tiled=True)  27 us
    all_to_all x4, starting transfers between devices, exchange(): lax.all_to_all(blocks, ('z', 'c'), split_axis=0, concat_axis=0, tiled=True)  25.4 us
    ppermute x12, starting transfers between devices, shift(): return lax.ppermute(a, axis, [(i, (i + step) % n) for i in range(n)])  14.2 us
    pallas_call x2, Pallas kernels, combine(): pl.pallas_call(combine_kernel, grid_spec=pltpu.PrefetchScalarGridSpec(num...  12.2 us
    ppermute x5, starting transfers between devices, swap_core(): return lax.ppermute(a, 'c', [(0, 1), (1, 0)])  8.67 us
    pallas_call x2, Pallas kernels, middle(): pl.pallas_call(functools.partial(kernel, lo, hi), grid=(N_X,), in_specs=[...  7.67 us
    ppermute x10, waiting for transfers between devices, swap(): lax.ppermute(a, axis, [(i, i ^ bits) for i in range(lax.axis_size(axis))])  7.56 us
  transfers between devices with their start and end apart: 31, of which 11 were waited for; matrix products, arithmetic and copies ran while one was open for 3% of the time, Pallas kernels for 29%

commit v1 on v0

--- a/solution.py
+++ b/solution.py
@@ -67,6 +67,17 @@
     )
 
 
+HEAD = 8 * CAP
+
+
+def table_lanes(packed):
+    l = iota((1, N_Z * packed), 1)
+    tail = packed - HEAD
+    low = l < N_Z * HEAD
+    rest = l - N_Z * HEAD
+    return jnp.where(low, l // HEAD, rest // tail), jnp.where(low, l % HEAD, HEAD + rest % tail)
+
+
 def select_kernel(scaled, with_tab, x_ref, ids_ref, w_ref, *refs):
     del x_ref
     segs, refs = refs[:N_X], refs[N_X:]
@@ -74,28 +85,25 @@
     if with_tab:
         (out_tab, in_tab), refs = refs[:2], refs[2:]
     sel_ref, row_ref = refs
-    tok = ids_ref.shape[0]
+    tok = ids_ref.shape[1]
     packed = send_ref.shape[2]
     blocks = packed // CAP
 
     @pl.when(pl.program_id(0) == 0)
     def _():
-        lane = iota((tok, 128), 1)
-        named = jnp.zeros((tok, 128), F32)
-        weight = jnp.zeros((tok, 128), F32)
-        for k in range(ids_ref.shape[1]):
-            hit = ids_ref[:, k : k + 1] == lane
+        expert = iota((128, tok), 0)
+        named = jnp.zeros((128, tok), F32)
+        weight_t = jnp.zeros((128, tok), F32)
+        for k in range(ids_ref.shape[0]):
+            hit = ids_ref[k : k + 1, :] == expert
             named = jnp.where(hit, 1.0, named)
-            weight = jnp.where(hit, w_ref[:, k : k + 1], weight)
-        earlier = jnp.where(iota((tok, tok), 1) < iota((tok, tok), 0), 1.0, 0.0).astype(BF)
-        place = dot_nn(earlier, named.astype(BF))
-        code = jnp.where(named > 0, place + 1.0, 0.0)
-        code_t = code.T
-        weight_t = weight.T
+            weight_t = jnp.where(hit, w_ref[k : k + 1, :], weight_t)
+        earlier = jnp.where(iota((tok, tok), 0) < iota((tok, tok), 1), 1.0, 0.0).astype(BF)
+        place = dot_nn(named.astype(BF), earlier)
+        code_t = jnp.where(named > 0, place + 1.0, 0.0)
         r = iota((packed, 1), 0)
         slot = (r % CAP + 1).astype(F32)
-        shape = (packed, blocks * tok)
-        diag = iota(shape, 0) // CAP == iota(shape, 1) // tok
+        diag = r // CAP == iota((1, blocks * tok), 1) // tok
         for e in range(N_Z):
             block = pl.ds(e * packed, packed)
             picked = jnp.broadcast_to(code_t[e : e + 1, :], (packed, tok)) == slot
@@ -107,12 +115,13 @@
                 row_ref[block, :] = jnp.broadcast_to(jnp.sum(part, axis=1, keepdims=True), (packed, 128))
         if with_tab:
             total = N_Z * packed
-            l = iota((128, total), 1)
-            spread = jnp.where(l // packed == iota((128, total), 0), 1.0, 0.0).astype(BF)
-            l = iota((tok, total), 1) % packed
-            valid = (dot_nn(code.astype(BF), spread) == (l % CAP + 1).astype(F32)) & (l < blocks * CAP)
+            code, weight = code_t.T.astype(BF), weight_t.T.astype(BF)
+            e, r = table_lanes(packed)
+            spread = jnp.where(e == iota((128, 1), 0), 1.0, 0.0).astype(BF)
+            slot = jnp.where(r < blocks * CAP, (r % CAP + 1).astype(F32), -1.0)
+            valid = dot_nn(code, spread) == slot
             in_tab[...] = jnp.where(valid, 1.0, 0.0).astype(BF)
-            out_tab[...] = jnp.where(valid, dot_nn(weight.astype(BF), spread), 0.0).astype(BF)
+            out_tab[...] = jnp.where(valid, dot_nn(weight, spread), 0.0).astype(BF)
 
     wide = jnp.concatenate([s[...] for s in segs], axis=1)
     stack = jnp.concatenate([wide[:, q * BLK : (q + 1) * BLK] for q in range(blocks)], axis=0)
@@ -158,7 +167,7 @@
             ],
         ),
         out_shape=out_shape,
-        compiler_params=params(SHARE),
+        compiler_params=params(ROOM),
         cost_estimate=cost(COST),
         name="select_cot" if scaled else "select_tok",
     )(x, ids, weights, *([data] * N_X))
@@ -170,8 +179,7 @@
 def unpack_kernel(in_ref, out_ref):
     packed = in_ref.shape[1]
     blocks = packed // CAP
-    shape = (blocks * GROWS, N_Z * packed)
-    row, col = iota(shape, 0), iota(shape, 1)
+    row, col = iota((blocks * GROWS, 1), 0), iota((1, N_Z * packed), 1)
     place = row % GROWS
     want = place // CAP * packed + row // GROWS * CAP + place % CAP
     perm = jnp.where(col == want, 1.0, 0.0).astype(BF)
@@ -203,11 +211,10 @@
     stack = jnp.concatenate(
         [total[:, q * BLK : (q + 1) * BLK] for q in range(blocks)], axis=0
     ).astype(BF)
-    shape = (N_Z * packed, blocks * GROWS)
-    row, col = iota(shape, 0), iota(shape, 1)
+    row, col = iota((N_Z * packed, 1), 0), iota((1, blocks * GROWS), 1)
     r = row % packed
     want = r // CAP * GROWS + row // packed * CAP + r % CAP
-    perm = jnp.where((col == want) & (r < blocks * CAP), 1.0, 0.0).astype(BF)
+    perm = jnp.where(col == jnp.where(r < blocks * CAP, want, -1), 1.0, 0.0).astype(BF)
     send_ref[...] = dot_nn(perm, stack).astype(BF).reshape(send_ref.shape)
 
 
@@ -226,36 +233,36 @@
     )(*parts)
 
 
-GROUP = 7
-
-
-def combine_kernel(x_ref, tab_ref, back_ref, out_ref, big_ref, acc_ref):
+def combine_kernel(x_ref, tab_ref, back_ref, out_ref, head_ref, tail_ref, acc_ref):
     del x_ref
     c, k = pl.program_id(0), pl.program_id(1)
     tok, total = tab_ref.shape
     packed = back_ref.shape[2]
-    blocks = packed // CAP
     seg = out_ref.shape[1]
+    heads = HEAD // CAP
+    tails = packed // CAP - heads
+    cut = N_Z * HEAD
 
     @pl.when((c == 0) & (k == 0))
     def _():
-        where = iota((tok, total), 1) % packed // CAP
-        for q in range(blocks):
-            big_ref[pl.ds(q * tok, tok), :] = jnp.where(where == q, tab_ref[...], jnp.zeros((), BF))
+        block = table_lanes(packed)[1] // CAP
+        for q in range(heads):
+            here = jnp.where(block[:, :cut] == q, 1.0, 0.0).astype(BF)
+            head_ref[pl.ds(q * tok, tok), :] = tab_ref[:, :cut] * here
+        for q in range(tails):
+            here = jnp.where(block[:, cut:] == heads + q, 1.0, 0.0).astype(BF)
+            tail_ref[pl.ds(q * tok, tok), :] = tab_ref[:, cut:] * here
 
     @pl.when(k == 0)
     def _():
-        back = back_ref[...].reshape(total, BLK)
-
-        def block(i, carry):
-            span = pl.ds(pl.multiple_of(i * GROUP * tok, tok), GROUP * tok)
-            out = dot_nn(big_ref[span, :], back).astype(BF)
-            for q in range(GROUP):
-                cols = pl.ds(pl.multiple_of((i * GROUP + q) * BLK, BLK), BLK)
-                acc_ref[:, cols] = out[q * tok : (q + 1) * tok]
-            return carry
-
-        lax.fori_loop(0, blocks // GROUP, block, 0)
+        back = back_ref[:, 0]
+        for ref, first, count, rows in (
+            (head_ref, 0, heads, back[:, :HEAD]),
+            (tail_ref, heads, tails, back[:, HEAD:]),
+        ):
+            out = dot_nn(ref[...], rows.reshape(ref.shape[1], BLK)).astype(BF)
+            for q in range(count):
+                acc_ref[:, pl.ds((first + q) * BLK, BLK)] = out[q * tok : (q + 1) * tok]
 
     for j in range(N_X):
 
@@ -282,7 +289,8 @@
                 (tok, seg), lambda c, k, x: (0, lax.bitwise_xor(x[0], k) * N_C + c)
             ),
             scratch_shapes=[
-                pltpu.VMEM((packed // CAP * tok, total), BF),
+                pltpu.VMEM((HEAD // CAP * tok, N_Z * HEAD), BF),
+                pltpu.VMEM(((packed // CAP - HEAD // CAP) * tok, total - N_Z * HEAD), BF),
                 pltpu.VMEM((tok, width // N_C), BF),
             ],
         ),
@@ -624,20 +632,21 @@
     core = lax.axis_index("c").reshape(1)
     merge = lambda a: a.reshape((N_Z * N_C,) + a.shape[2:])
 
+    route_ids, router_weights = route_ids.T, router_weights.T
     tok_send, out_tab, in_tab = select(x, route_ids, router_weights, tokens, False, True)
     tok_packed = exchange(merge(tok_send))
     (cot_send,) = select(x, route_ids, router_weights, after(cotangent, tok_send), True, False)
     cot_packed = exchange(merge(cot_send))
 
-    own, give = split_master(core, master)
+    own, give = split_master(core, after(master, cot_send))
     got = swap_core(give)
     own_weights = gather_x(own, 1)
     got_weights = gather_x(got, 3)
     weights = [w for pair in zip(own_weights, got_weights) for w in pair]
 
-    tok_packed = after(tok_packed, own_weights[1], own_weights[3])
+    tok_packed = after(tok_packed, cot_send, got)
     tok_rows = gather_y(unpack(tok_packed), 1)
-    cot_packed = after(cot_packed, tok_rows[1], tok_rows[3], got_weights[1], got_weights[3])
+    cot_packed = after(cot_packed, tok_rows[1], got_weights[1], got_weights[3])
     cot_rows = gather_y(unpack(cot_packed), -1)
 
     pre = project(tok_rows, weights, 0, 2 * hid)

time: 196 us -> 192 us (0.980)
  waiting for transfers between devices: 68.2 us -> 54.3 us
  starting transfers between devices: 55.8 us -> 66.6 us
    all_to_all x4, waiting for transfers between devices: 27 us -> 10.1 us  [exchange(): lax.all_to_all(blocks, ('z', 'c'), split_axis=0, concat_axis=0, tiled=True)]
    ppermute x10, waiting for transfers between devices: 7.56 us -> 17.7 us  [swap(): lax.ppermute(a, axis, [(i, i ^ bits) for i in range(lax.axis_size(axis))])]
    ppermute x12, waiting for transfers between devices: 33.6 us -> 26.4 us  [shift(): return lax.ppermute(a, axis, [(i, (i + step) % n) for i in range(n)])]
    ppermute x10, starting transfers between devices: 7.5 us -> 13.7 us  [swap(): lax.ppermute(a, axis, [(i, i ^ bits) for i in range(lax.axis_size(axis))])]
    pallas_call x2, Pallas kernels: 12.2 us -> 10.1 us  [combine(): pl.pallas_call(combine_kernel, grid_spec=pltpu.PrefetchScalarGridSpec(num...]
    ppermute x12, starting transfers between devices: 14.2 us -> 16.1 us  [shift(): return lax.ppermute(a, axis, [(i, (i + step) % n) for i in range(n)])]
  transfers between devices with their start and end apart: 31 -> 31, of which waited for: 11 -> 10; matrix products, arithmetic and copies ran while one was open for 3% -> 3% of each run, Pallas kernels for 29% -> 30%
where the time goes in v1:
time: 192 us; the launch traced here: 191 us
  starting transfers between devices  66.6 us (35%)
  Pallas kernels  62 us (32%)
  waiting for transfers between devices  54.3 us (28%)
  other arithmetic  5.76 us (3%)
    all_to_all x4, starting transfers between devices, exchange(): lax.all_to_all(blocks, ('z', 'c'), split_axis=0, concat_axis=0, tiled=True)  27.2 us
    ppermute x12, waiting for transfers between devices, shift(): return lax.ppermute(a, axis, [(i, (i + step) % n) for i in range(n)])  26.4 us
    ppermute x10, waiting for transfers between devices, swap(): lax.ppermute(a, axis, [(i, i ^ bits) for i in range(lax.axis_size(axis))])  17.7 us
    ppermute x12, starting transfers between devices, shift(): return lax.ppermute(a, axis, [(i, (i + step) % n) for i in range(n)])  16.1 us
    ppermute x10, starting transfers between devices, swap(): lax.ppermute(a, axis, [(i, i ^ bits) for i in range(lax.axis_size(axis))])  13.7 us
    all_to_all x4, waiting for transfers between devices, exchange(): lax.all_to_all(blocks, ('z', 'c'), split_axis=0, concat_axis=0, tiled=True)  10.1 us
    pallas_call x2, Pallas kernels, combine(): pl.pallas_call(combine_kernel, grid_spec=pltpu.PrefetchScalarGridSpec(num...  10.1 us
    ppermute x5, starting transfers between devices, swap_core(): return lax.ppermute(a, 'c', [(0, 1), (1, 0)])  9.63 us
  transfers between devices with their start and end apart: 31, of which 10 were waited for; matrix products, arithmetic and copies ran while one was open for 3% of the time, Pallas kernels for 30%

profile of v1, /device:TPU:1, one launch (start us, length us, event | category | flops | bytes accessed | tf_op | source)
XLA Modules:
  0.0 191.2 jit_solution(3228475680052706581)
XLA Ops:
  0.6 4.4 %select_tok.1 = (bf16[8,2,72,256]{3,2,1,0:T(8,128)(2,1)}, bf16[128,576]{1,0:T(8,128)(2,1)}, bf16[128,576]{1,0:T(8,128)(2,1)}) custom-call(s32[1]{0:T(128)} %bitcast.x_ref, s32[8,128]{1,0:T(8,128)} %bitcast.25, f32[8,128]{1,0:T(8,128)} %bitcast.27, bf16[128,7168]{1,0:T(8,128)(2,1)} %refs_3_.1, bf16[128,7168]{1,0:T(8,128)(2,1)} %refs_3_.1, ...), custom_call_target="tpu_custom_call" | custom-call | flops 99999997952 | bytes 100000000 | tf_op jit(solution)/shard_map/select_tok/pallas_call | solution.py:153
  5.0 10.0 %all-to-all-start = ((bf16[16,72,256]{2,1,0:T(8,128)(2,1)}), bf16[16,72,256]{2,1,0:T(8,128)(2,1)}, u32[]{:S(2)}, u32[]{:S(2)}) async-start(bf16[16,72,256]{2,1,0:T(8,128)(2,1)} %bitcast.24), calls=%async_computation | async-start | bytes 1179648 | tf_op jit(solution)/shard_map/all_to_all | solution.py:626
  15.0 4.2 %select_cot.1 = bf16[8,2,72,256]{3,2,1,0:T(8,128)(2,1)} custom-call(s32[1]{0:T(128)} %bitcast.x_ref, s32[8,128]{1,0:T(8,128)} %bitcast.26, f32[8,128]{1,0:T(8,128)} %bitcast.28, bf16[128,7168]{1,0:T(8,128)(2,1)} %refs_3_.2, bf16[128,7168]{1,0:T(8,128)(2,1)} %refs_3_.2, bf16[128,7168]{1,0:T(8,128)(2,1)} %refs_3_.2, bf16[128,7168]{1,0:T(8,128)(2,1)} %refs_3_.2), custom_call_target="tpu_custom_call" | custom-call | flops 99999997952 | bytes 100000000 | tf_op jit(solution)/shard_map/select_cot/pallas_call | solution.py:153
  27.4 6.3 %all-to-all-done.in_ref = bf16[16,72,256]{2,1,0:T(8,128)(2,1)} async-done(((bf16[16,72,256]{2,1,0:T(8,128)(2,1)}), bf16[16,72,256]{2,1,0:T(8,128)(2,1)}, u32[]{:S(2)}, u32[]{:S(2)}) %all-to-all-start) | async-done | bytes 589856 | tf_op jit(solution)/shard_map/all_to_all | solution.py:626
  33.8 3.5 %all-to-all-start.2 = ((bf16[16,72,256]{2,1,0:T(8,128)(2,1)}), bf16[16,72,256]{2,1,0:T(8,128)(2,1)S(1)}, u32[]{:S(2)}, u32[]{:S(2)}) async-start(bf16[16,72,256]{2,1,0:T(8,128)(2,1)} %bitcast.6), calls=%async_computation.2 | async-start | bytes 1179648 | tf_op jit(solution)/shard_map/all_to_all | solution.py:626
  44.6 10.6 %collective-permute-done.9.refs_11_.refs_7_ = bf16[896,384]{1,0:T(8,128)(2,1)} collective-permute-done((bf16[896,384]{1,0:T(8,128)(2,1)S(1)}, bf16[896,384]{1,0:T(8,128)(2,1)}, u32[]{:S(2)}, u32[]{:S(2)}) %collective-permute-start.9) | collective-permute-done | bytes 688160 | tf_op jit(solution)/shard_map/ppermute | solution.py:28
  62.2 10.5 %collective-permute-done.14.refs_1_.refs_5_ = bf16[80,3584]{1,0:T(8,128)(2,1)S(1)} collective-permute-done((bf16[80,3584]{1,0:T(8,128)(2,1)S(1)}, bf16[80,3584]{1,0:T(8,128)(2,1)S(1)}, u32[]{:S(2)}, u32[]{:S(2)}) %collective-permute-start.14) | collective-permute-done | bytes 573472 | tf_op jit(solution)/shard_map/ppermute | solution.py:33
  72.7 3.5 %collective-permute-start.15 = (bf16[80,3584]{1,0:T(8,128)(2,1)S(1)}, bf16[80,3584]{1,0:T(8,128)(2,1)S(1)}, u32[]{:S(2)}, u32[]{:S(2)}) collective-permute-start(bf16[80,3584]{1,0:T(8,128)(2,1)S(1)} %collective-permute-done.14.refs_1_.refs_5_), channel_id=1, source_target_pairs={{0,6},{2,0},{4,2},{6,4},{1,7},{3,1},{5,3},{7,5},{8,14},{10,8},{12,... | collective-permute-start | bytes 1720328 | tf_op jit(solution)/shard_map/ppermute | solution.py:33
  76.2 4.7 %project_rows.2.half_ref = f32[320,512]{1,0:T(8,128)S(1)} custom-call(bf16[80,3584]{1,0:T(8,128)(2,1)} %unpack_rows.2.refs_0_, bf16[80,3584]{1,0:T(8,128)(2,1)} %collective-permute-done.1.refs_1_, bf16[80,3584]{1,0:T(8,128)(2,1)S(1)} %collective-permute-done.3.refs_2_, bf16[80,3584]{1,0:T(8,128)(2,1)} %collective-permute-done.2.refs_3_, ...), custom_call_target="tpu_custom_call" | custom-call | flops 99999997952 | bytes 100000000 | tf_op jit(solution)/shard_map/project_rows/pallas_call | solution.py:384
  81.0 4.8 %collective-permute-start.10 = (f32[320,512]{1,0:T(8,128)S(1)}, f32[320,512]{1,0:T(8,128)S(1)}, u32[]{:S(2)}, u32[]{:S(2)}) collective-permute-start(f32[320,512]{1,0:T(8,128)S(1)} %project_rows.2.half_ref), channel_id=1, source_target_pairs={{0,1},{1,0},{2,3},{3,2},{4,5},{5,4},{6,7},{7,6},{8,9},{9,8},{10,11... | collective-permute-start | bytes 1966088 | tf_op jit(solution)/shard_map/ppermute | solution.py:24
  93.8 3.5 %forward_rows.1 = (bf16[320,256]{1,0:T(8,128)(2,1)S(1)}, bf16[80,3584]{1,0:T(8,128)(2,1)S(1)}, bf16[80,3584]{1,0:T(8,128)(2,1)}, bf16[80,3584]{1,0:T(8,128)(2,1)}, bf16[80,3584]{1,0:T(8,128)(2,1)}) custom-call(f32[320,512]{1,0:T(8,128)S(1)} %project_rows.2.half_ref, f32[320,512]{1,0:T(8,128)S(1)} %collective-permute-done.10.other_ref, ...), custom_call_target="tpu_custom_call" | custom-call | flops 99999997952 | bytes 100000000 | tf_op jit(solution)/shard_map/forward_rows/pallas_call | solution.py:451
  100.3 4.2 %backward_rows.1 = (bf16[320,512]{1,0:T(8,128)(2,1)S(1)}, bf16[80,3584]{1,0:T(8,128)(2,1)S(1)}, bf16[80,3584]{1,0:T(8,128)(2,1)}, bf16[80,3584]{1,0:T(8,128)(2,1)}, bf16[80,3584]{1,0:T(8,128)(2,1)}) custom-call(f32[320,512]{1,0:T(8,128)S(1)} %project_rows.2.half_ref, f32[320,512]{1,0:T(8,128)S(1)} %collective-permute-done.10.other_ref, ...), custom_call_target="tpu_custom_call" | custom-call | flops 99999997952 | bytes 100000000 | tf_op jit(solution)/shard_map/backward_rows/pallas_call | solution.py:451
  104.5 7.2 %weight_grad.1 = (bf16[896,384]{1,0:T(8,128)(2,1)S(1)}, bf16[2,896,384]{2,1,0:T(8,128)(2,1)}, bf16[896,384]{1,0:T(8,128)(2,1)S(1)}, bf16[896,384]{1,0:T(8,128)(2...) custom-call(bf16[320,256]{1,0:T(8,128)(2,1)S(1)} %get-tuple-element.50.hidden_ref, ...), custom_call_target="tpu_custom_call" | custom-call | flops 99999997952 | bytes 100000000 | tf_op jit(solution)/shard_map/weight_grad/pallas_call | solution.py:503
  116.7 9.7 %collective-permute-done.12.refs_2_ = bf16[80,3584]{1,0:T(8,128)(2,1)} collective-permute-done((bf16[80,3584]{1,0:T(8,128)(2,1)}, bf16[80,3584]{1,0:T(8,128)(2,1)}, u32[]{:S(2)}, u32[]{:S(2)}) %collective-permute-start.12) | collective-permute-done | bytes 573472 | tf_op jit(solution)/shard_map/ppermute | solution.py:33
  129.0 3.6 %pack_rows.2 = bf16[16,72,256]{2,1,0:T(8,128)(2,1)} custom-call(bf16[80,3584]{1,0:T(8,128)(2,1)S(1)} %get-tuple-element.44.refs_0_, bf16[80,3584]{1,0:T(8,128)(2,1)} %collective-permute-done.11.refs_1_, bf16[80,3584]{1,0:T(8,128)(2,1)} %collective-permute-done.12.refs_2_, bf16[80,3584]{1,0:T(8,128)(2,1)} %collective-permute-done.13.refs_3_), custom_call_target="tpu_custom_call" | custom-call | flops 99999997952 | bytes 100000000 | tf_op jit(solution)/shard_map/pack_rows/pallas_call | solution.py:224
  132.6 8.8 %all-to-all-start.1 = ((bf16[16,72,256]{2,1,0:T(8,128)(2,1)}), bf16[16,72,256]{2,1,0:T(8,128)(2,1)S(1)}, u32[]{:S(2)}, u32[]{:S(2)}) async-start(bf16[16,72,256]{2,1,0:T(8,128)(2,1)} %pack_rows.2), calls=%async_computation.1 | async-start | bytes 1179648 | tf_op jit(solution)/shard_map/all_to_all | solution.py:626
  141.4 3.8 %collective-permute-done.21 = bf16[2,896,384]{2,1,0:T(8,128)(2,1)} collective-permute-done((bf16[2,896,384]{2,1,0:T(8,128)(2,1)}, bf16[2,896,384]{2,1,0:T(8,128)(2,1)}, u32[]{:S(2)}, u32[]{:S(2)}) %collective-permute-start.21) | collective-permute-done | bytes 1376288 | tf_op jit(solution)/shard_map/ppermute | solution.py:28
  147.4 3.7 %collective-permute-done.19.refs_2_ = bf16[80,3584]{1,0:T(8,128)(2,1)} collective-permute-done((bf16[80,3584]{1,0:T(8,128)(2,1)}, bf16[80,3584]{1,0:T(8,128)(2,1)}, u32[]{:S(2)}, u32[]{:S(2)}) %collective-permute-start.19) | collective-permute-done | bytes 573472 | tf_op jit(solution)/shard_map/ppermute | solution.py:33
  151.0 3.5 %pack_rows.3 = bf16[16,72,256]{2,1,0:T(8,128)(2,1)} custom-call(bf16[80,3584]{1,0:T(8,128)(2,1)S(1)} %copy-done.15, bf16[80,3584]{1,0:T(8,128)(2,1)S(1)} %collective-permute-done.18.refs_1_, bf16[80,3584]{1,0:T(8,128)(2,1)} %collective-permute-done.19.refs_2_, bf16[80,3584]{1,0:T(8,128)(2,1)} %collective-permute-done.20.refs_3_), custom_call_target="tpu_custom_call" | custom-call | flops 99999997952 | bytes 100000000 | tf_op jit(solution)/shard_map/pack_rows/pallas_call | solution.py:224
  160.1 4.9 %all-to-all-start.3 = ((bf16[16,72,256]{2,1,0:T(8,128)(2,1)}), bf16[16,72,256]{2,1,0:T(8,128)(2,1)}, u32[]{:S(2)}, u32[]{:S(2)}) async-start(bf16[16,72,256]{2,1,0:T(8,128)(2,1)} %pack_rows.3), calls=%async_computation.3 | async-start | bytes 1179648 | tf_op jit(solution)/shard_map/all_to_all | solution.py:626
  167.0 4.4 %combine_rows.2 = bf16[128,7168]{1,0:T(8,128)(2,1)} custom-call(s32[1]{0:T(128)} %bitcast.x_ref, bf16[128,576]{1,0:T(8,128)(2,1)S(1)} %copy-done.17, bf16[8,2,72,256]{3,2,1,0:T(8,128)(2,1)S(1)} %bitcast.23), custom_call_target="tpu_custom_call" | custom-call | flops 99999997952 | bytes 100000000 | tf_op jit(solution)/shard_map/combine_rows/pallas_call | solution.py:279
  171.4 3.3 %collective-permute-done.25.refs_2_ = bf16[896,384]{1,0:T(8,128)(2,1)S(1)} collective-permute-done((bf16[896,384]{1,0:T(8,128)(2,1)}, bf16[896,384]{1,0:T(8,128)(2,1)S(1)}, u32[]{:S(2)}, u32[]{:S(2)}) %collective-permute-start.25) | collective-permute-done | bytes 688160 | tf_op jit(solution)/shard_map/ppermute | solution.py:28
  174.7 5.5 %update_master.1 = (bf16[1792,384]{1,0:T(8,128)(2,1)S(1)}, f32[1,3,1792]{2,1,0:T(4,128)S(1)}) custom-call(s32[1]{0:T(128)} %bitcast.4.c_ref, f32[1,1792,384]{2,1,0:T(8,128)S(1)} %copy-done, f32[1,3,1792]{2,1,0:T(4,128)S(1)} %copy.10.sums_ref, bf16[896,384]{1,0:T(8,128)(2,1)S(1)} %collective-permute-done.23.other_ref, bf16[896,384]{1,0:T(8,128)(2,1)S(1)} %copy-done.13, ...), custom_call_target="tpu_custom_call" | custom-call | flops 99999997952 | bytes 100000000 | tf_op jit(solution)/shard_map/update_master/pallas_call | solution.py:590
  183.7 5.7 %combine_rows.3 = bf16[128,7168]{1,0:T(8,128)(2,1)} custom-call(s32[1]{0:T(128)} %bitcast.x_ref, bf16[128,576]{1,0:T(8,128)(2,1)S(1)} %copy-done.16, bf16[8,2,72,256]{3,2,1,0:T(8,128)(2,1)} %bitcast.7.back_ref), custom_call_target="tpu_custom_call" | custom-call | flops 99999997952 | bytes 100000000 | tf_op jit(solution)/shard_map/combine_rows/pallas_call | solution.py:279
  (97 shorter events, 56.1 us)
Async XLA Ops:
  5.0 28.8 %all-to-all-start = ((bf16[16,72,256]{2,1,0:T(8,128)(2,1)}), bf16[16,72,256]{2,1,0:T(8,128)(2,1)}, u32[]{:S(2)}, u32[]{:S(2)}) async-start(bf16[16,72,256]{2,1,0:T(8,128)(2,1)} %bitcast.24), calls=%async_computation | async-start | bytes 1179648 | tf_op jit(solution)/shard_map/all_to_all | solution.py:626
  22.2 22.1 %collective-permute-start.6 = (bf16[896,384]{1,0:T(8,128)(2,1)}, bf16[896,384]{1,0:T(8,128)(2,1)S(1)}, u32[]{:S(2)}, u32[]{:S(2)}) collective-permute-start(bf16[896,384]{1,0:T(8,128)(2,1)} %get-tuple-element.43.refs_4_.refs_0_), channel_id=1, source_target_pairs={{0,192},{64,128},{128,64},{192,0},{1,193},{65,129},{129,65},{193,1... | collective-permute-start | bytes 2064392 | tf_op jit(solution)/shard_map/ppermute | solution.py:28
  24.7 19.9 %collective-permute-start.5 = (bf16[896,384]{1,0:T(8,128)(2,1)S(1)}, bf16[896,384]{1,0:T(8,128)(2,1)S(1)}, u32[]{:S(2)}, u32[]{:S(2)}) collective-permute-start(bf16[896,384]{1,0:T(8,128)(2,1)S(1)} %collective-permute-done.refs_5_.refs_1_), channel_id=1, source_target_pairs={{0,64},{64,0},{128,192},{192,128},{1,65},{65,1},{129,193},{193,129... | collective-permute-start | bytes 2064392 | tf_op jit(solution)/shard_map/ppermute | solution.py:28
  25.6 29.5 %collective-permute-start.9 = (bf16[896,384]{1,0:T(8,128)(2,1)S(1)}, bf16[896,384]{1,0:T(8,128)(2,1)}, u32[]{:S(2)}, u32[]{:S(2)}) collective-permute-start(bf16[896,384]{1,0:T(8,128)(2,1)S(1)} %collective-permute-done.refs_5_.refs_1_), channel_id=1, source_target_pairs={{0,192},{64,128},{128,64},{192,0},{1,193},{65,129},{129,65},{193,1... | collective-permute-start | bytes 2064392 | tf_op jit(solution)/shard_map/ppermute | solution.py:28
  33.8 23.9 %all-to-all-start.2 = ((bf16[16,72,256]{2,1,0:T(8,128)(2,1)}), bf16[16,72,256]{2,1,0:T(8,128)(2,1)S(1)}, u32[]{:S(2)}, u32[]{:S(2)}) async-start(bf16[16,72,256]{2,1,0:T(8,128)(2,1)} %bitcast.6), calls=%async_computation.2 | async-start | bytes 1179648 | tf_op jit(solution)/shard_map/all_to_all | solution.py:626
  40.4 17.3 %collective-permute-start.1 = (bf16[80,3584]{1,0:T(8,128)(2,1)}, bf16[80,3584]{1,0:T(8,128)(2,1)}, u32[]{:S(2)}, u32[]{:S(2)}) collective-permute-start(bf16[80,3584]{1,0:T(8,128)(2,1)} %unpack_rows.2.refs_0_), channel_id=1, source_target_pairs={{0,6},{2,0},{4,2},{6,4},{1,7},{3,1},{5,3},{7,5},{8,14},{10,8},{12,... | collective-permute-start | bytes 1720328 | tf_op jit(solution)/shard_map/ppermute | solution.py:33
  43.1 18.8 %collective-permute-start.4 = (bf16[896,384]{1,0:T(8,128)(2,1)S(1)}, bf16[896,384]{1,0:T(8,128)(2,1)}, u32[]{:S(2)}, u32[]{:S(2)}) collective-permute-start(bf16[896,384]{1,0:T(8,128)(2,1)S(1)} %copy-done.1), channel_id=1, source_target_pairs={{0,64},{64,0},{128,192},{192,128},{1,65},{65,1},{129,193},{193,129... | collective-permute-start | bytes 2064392 | tf_op jit(solution)/shard_map/ppermute | solution.py:28
  44.3 31.9 %collective-permute-start.7 = (bf16[896,384]{1,0:T(8,128)(2,1)S(1)}, bf16[896,384]{1,0:T(8,128)(2,1)}, u32[]{:S(2)}, u32[]{:S(2)}) collective-permute-start(bf16[896,384]{1,0:T(8,128)(2,1)S(1)} %collective-permute-done.6.refs_10_.refs_6_), channel_id=1, source_target_pairs={{0,64},{64,0},{128,192},{192,128},{1,65},{65,1},{129,193},{193,129... | collective-permute-start | bytes 2064392 | tf_op jit(solution)/shard_map/ppermute | solution.py:28
  44.6 17.3 %collective-permute-start.2 = (bf16[80,3584]{1,0:T(8,128)(2,1)}, bf16[80,3584]{1,0:T(8,128)(2,1)}, u32[]{:S(2)}, u32[]{:S(2)}) collective-permute-start(bf16[80,3584]{1,0:T(8,128)(2,1)} %unpack_rows.2.refs_0_), channel_id=1, source_target_pairs={{0,2},{2,4},{4,6},{6,0},{1,3},{3,5},{5,7},{7,1},{8,10},{10,12},{12... | collective-permute-start | bytes 1720328 | tf_op jit(solution)/shard_map/ppermute | solution.py:33
  55.2 21.0 %collective-permute-start.8 = (bf16[896,384]{1,0:T(8,128)(2,1)S(1)}, bf16[896,384]{1,0:T(8,128)(2,1)}, u32[]{:S(2)}, u32[]{:S(2)}) collective-permute-start(bf16[896,384]{1,0:T(8,128)(2,1)S(1)} %collective-permute-done.5.refs_7_.refs_3_), channel_id=1, source_target_pairs={{0,192},{64,128},{128,64},{192,0},{1,193},{65,129},{129,65},{193,1... | collective-permute-start | bytes 2064392 | tf_op jit(solution)/shard_map/ppermute | solution.py:28
  61.9 26.4 %collective-permute-start.16 = (bf16[80,3584]{1,0:T(8,128)(2,1)S(1)}, bf16[80,3584]{1,0:T(8,128)(2,1)S(1)}, u32[]{:S(2)}, u32[]{:S(2)}) collective-permute-start(bf16[80,3584]{1,0:T(8,128)(2,1)S(1)} %unpack_rows.3.refs_0_.refs_4_), channel_id=1, source_target_pairs={{0,2},{2,4},{4,6},{6,0},{1,3},{3,5},{5,7},{7,1},{8,10},{10,12},{12... | collective-permute-start | bytes 1720328 | tf_op jit(solution)/shard_map/ppermute | solution.py:33
  72.7 15.6 %collective-permute-start.15 = (bf16[80,3584]{1,0:T(8,128)(2,1)S(1)}, bf16[80,3584]{1,0:T(8,128)(2,1)S(1)}, u32[]{:S(2)}, u32[]{:S(2)}) collective-permute-start(bf16[80,3584]{1,0:T(8,128)(2,1)S(1)} %collective-permute-done.14.refs_1_.refs_5_), channel_id=1, source_target_pairs={{0,6},{2,0},{4,2},{6,4},{1,7},{3,1},{5,3},{7,5},{8,14},{10,8},{12,... | collective-permute-start | bytes 1720328 | tf_op jit(solution)/shard_map/ppermute | solution.py:33
  97.3 18.2 %collective-permute-start.11 = (bf16[80,3584]{1,0:T(8,128)(2,1)}, bf16[80,3584]{1,0:T(8,128)(2,1)}, u32[]{:S(2)}, u32[]{:S(2)}) collective-permute-start(bf16[80,3584]{1,0:T(8,128)(2,1)} %get-tuple-element.45), channel_id=1, source_target_pairs={{0,4},{2,6},{4,0},{6,2},{1,5},{3,7},{5,1},{7,3},{8,12},{10,14},{12... | collective-permute-start | bytes 1720328 | tf_op jit(solution)/shard_map/ppermute | solution.py:33
  97.6 28.7 %collective-permute-start.12 = (bf16[80,3584]{1,0:T(8,128)(2,1)}, bf16[80,3584]{1,0:T(8,128)(2,1)}, u32[]{:S(2)}, u32[]{:S(2)}) collective-permute-start(bf16[80,3584]{1,0:T(8,128)(2,1)} %get-tuple-element.46), channel_id=1, source_target_pairs={{0,2},{2,4},{4,6},{6,0},{1,3},{3,5},{5,7},{7,1},{8,10},{10,12},{12... | collective-permute-start | bytes 1720328 | tf_op jit(solution)/shard_map/ppermute | solution.py:33
  99.7 26.7 %collective-permute-start.13 = (bf16[80,3584]{1,0:T(8,128)(2,1)}, bf16[80,3584]{1,0:T(8,128)(2,1)}, u32[]{:S(2)}, u32[]{:S(2)}) collective-permute-start(bf16[80,3584]{1,0:T(8,128)(2,1)} %get-tuple-element.47), channel_id=1, source_target_pairs={{0,6},{2,0},{4,2},{6,4},{1,7},{3,1},{5,3},{7,5},{8,14},{10,8},{12,... | collective-permute-start | bytes 1720328 | tf_op jit(solution)/shard_map/ppermute | solution.py:33
  112.7 32.5 %collective-permute-start.21 = (bf16[2,896,384]{2,1,0:T(8,128)(2,1)}, bf16[2,896,384]{2,1,0:T(8,128)(2,1)}, u32[]{:S(2)}, u32[]{:S(2)}) collective-permute-start(bf16[2,896,384]{2,1,0:T(8,128)(2,1)} %get-tuple-element.55), channel_id=1, source_target_pairs={{0,192},{64,128},{128,64},{192,0},{1,193},{65,129},{129,65},{193,1... | collective-permute-start | bytes 4128776 | tf_op jit(solution)/shard_map/ppermute | solution.py:28
  115.5 39.0 %collective-permute-start.24 = (bf16[2,896,384]{2,1,0:T(8,128)(2,1)}, bf16[2,896,384]{2,1,0:T(8,128)(2,1)}, u32[]{:S(2)}, u32[]{:S(2)}) collective-permute-start(bf16[2,896,384]{2,1,0:T(8,128)(2,1)} %get-tuple-element.54), channel_id=1, source_target_pairs={{0,64},{64,0},{128,192},{192,128},{1,65},{65,1},{129,193},{193,129... | collective-permute-start | bytes 4128776 | tf_op jit(solution)/shard_map/ppermute | solution.py:28
  115.5 31.9 %collective-permute-start.18 = (bf16[80,3584]{1,0:T(8,128)(2,1)}, bf16[80,3584]{1,0:T(8,128)(2,1)S(1)}, u32[]{:S(2)}, u32[]{:S(2)}) collective-permute-start(bf16[80,3584]{1,0:T(8,128)(2,1)} %get-tuple-element.58), channel_id=1, source_target_pairs={{0,4},{2,6},{4,0},{6,2},{1,5},{3,7},{5,1},{7,3},{8,12},{10,14},{12... | collective-permute-start | bytes 1720328 | tf_op jit(solution)/shard_map/ppermute | solution.py:33
  126.3 24.7 %collective-permute-start.19 = (bf16[80,3584]{1,0:T(8,128)(2,1)}, bf16[80,3584]{1,0:T(8,128)(2,1)}, u32[]{:S(2)}, u32[]{:S(2)}) collective-permute-start(bf16[80,3584]{1,0:T(8,128)(2,1)} %get-tuple-element.60), channel_id=1, source_target_pairs={{0,2},{2,4},{4,6},{6,0},{1,3},{3,5},{5,7},{7,1},{8,10},{10,12},{12... | collective-permute-start | bytes 1720328 | tf_op jit(solution)/shard_map/ppermute | solution.py:33
  126.3 24.7 %collective-permute-start.20 = (bf16[80,3584]{1,0:T(8,128)(2,1)}, bf16[80,3584]{1,0:T(8,128)(2,1)}, u32[]{:S(2)}, u32[]{:S(2)}) collective-permute-start(bf16[80,3584]{1,0:T(8,128)(2,1)} %get-tuple-element.62), channel_id=1, source_target_pairs={{0,6},{2,0},{4,2},{6,4},{1,7},{3,1},{5,3},{7,5},{8,14},{10,8},{12,... | collective-permute-start | bytes 1720328 | tf_op jit(solution)/shard_map/ppermute | solution.py:33
  132.6 27.5 %all-to-all-start.1 = ((bf16[16,72,256]{2,1,0:T(8,128)(2,1)}), bf16[16,72,256]{2,1,0:T(8,128)(2,1)S(1)}, u32[]{:S(2)}, u32[]{:S(2)}) async-start(bf16[16,72,256]{2,1,0:T(8,128)(2,1)} %pack_rows.2), calls=%async_computation.1 | async-start | bytes 1179648 | tf_op jit(solution)/shard_map/all_to_all | solution.py:626
  147.4 17.6 %collective-permute-start.22 = (bf16[896,384]{1,0:T(8,128)(2,1)}, bf16[896,384]{1,0:T(8,128)(2,1)S(1)}, u32[]{:S(2)}, u32[]{:S(2)}) collective-permute-start(bf16[896,384]{1,0:T(8,128)(2,1)} %fusion.1), channel_id=1, source_target_pairs={{0,64},{64,0},{128,192},{192,128},{1,65},{65,1},{129,193},{193,129... | collective-permute-start | bytes 2064392 | tf_op jit(solution)/shard_map/ppermute | solution.py:28
  156.6 18.0 %collective-permute-start.25 = (bf16[896,384]{1,0:T(8,128)(2,1)}, bf16[896,384]{1,0:T(8,128)(2,1)S(1)}, u32[]{:S(2)}, u32[]{:S(2)}) collective-permute-start(bf16[896,384]{1,0:T(8,128)(2,1)} %fusion), channel_id=1, source_target_pairs={{0,192},{64,128},{128,64},{192,0},{1,193},{65,129},{129,65},{193,1... | collective-permute-start | bytes 2064392 | tf_op jit(solution)/shard_map/ppermute | solution.py:28
  160.1 23.6 %all-to-all-start.3 = ((bf16[16,72,256]{2,1,0:T(8,128)(2,1)}), bf16[16,72,256]{2,1,0:T(8,128)(2,1)}, u32[]{:S(2)}, u32[]{:S(2)}) async-start(bf16[16,72,256]{2,1,0:T(8,128)(2,1)} %pack_rows.3), calls=%async_computation.3 | async-start | bytes 1179648 | tf_op jit(solution)/shard_map/all_to_all | solution.py:626
  (26 other events, 218.7 us)

commit v2 on v1

--- a/solution.py
+++ b/solution.py
@@ -84,7 +84,7 @@
     send_ref, refs = refs[0], refs[1:]
     if with_tab:
         (out_tab, in_tab), refs = refs[:2], refs[2:]
-    sel_ref, row_ref = refs
+    head_ref, tail_ref, head_row, tail_row = refs
     tok = ids_ref.shape[1]
     packed = send_ref.shape[2]
     blocks = packed // CAP
@@ -101,18 +101,27 @@
         earlier = jnp.where(iota((tok, tok), 0) < iota((tok, tok), 1), 1.0, 0.0).astype(BF)
         place = dot_nn(named.astype(BF), earlier)
         code_t = jnp.where(named > 0, place + 1.0, 0.0)
-        r = iota((packed, 1), 0)
-        slot = (r % CAP + 1).astype(F32)
-        diag = r // CAP == iota((1, blocks * tok), 1) // tok
-        for e in range(N_Z):
-            block = pl.ds(e * packed, packed)
-            picked = jnp.broadcast_to(code_t[e : e + 1, :], (packed, tok)) == slot
-            ones = jnp.where(picked, 1.0, 0.0)
-            wide = jnp.concatenate([ones] * blocks, axis=1)
-            sel_ref[block, :] = jnp.where(diag, wide, 0.0).astype(BF)
-            if scaled:
-                part = jnp.where(picked, jnp.broadcast_to(weight_t[e : e + 1, :], (packed, tok)), 0.0)
-                row_ref[block, :] = jnp.broadcast_to(jnp.sum(part, axis=1, keepdims=True), (packed, 128))
+        for sel_ref, row_ref, count in (
+            (head_ref, head_row, HEAD),
+            (tail_ref, tail_row, packed - HEAD),
+        ):
+            r = iota((count, 1), 0)
+            slot = (r % CAP + 1).astype(F32)
+            columns = sel_ref.shape[1]
+            diag = r // CAP == iota((1, columns), 1) // tok
+            for e in range(N_Z):
+                span = pl.ds(e * count, count)
+                picked = jnp.broadcast_to(code_t[e : e + 1, :], (count, tok)) == slot
+                ones = jnp.where(picked, 1.0, 0.0)
+                wide = jnp.concatenate([ones] * (columns // tok), axis=1)
+                sel_ref[span, :] = jnp.where(diag, wide, 0.0).astype(BF)
+                if scaled:
+                    part = jnp.where(
+                        picked, jnp.broadcast_to(weight_t[e : e + 1, :], (count, tok)), 0.0
+                    )
+                    row_ref[span, :] = jnp.broadcast_to(
+                        jnp.sum(part, axis=1, keepdims=True), (count, 128)
+                    )
         if with_tab:
             total = N_Z * packed
             code, weight = code_t.T.astype(BF), weight_t.T.astype(BF)
@@ -124,11 +133,18 @@
             out_tab[...] = jnp.where(valid, dot_nn(weight, spread), 0.0).astype(BF)
 
     wide = jnp.concatenate([s[...] for s in segs], axis=1)
-    stack = jnp.concatenate([wide[:, q * BLK : (q + 1) * BLK] for q in range(blocks)], axis=0)
-    rows = dot_nn(sel_ref[...], stack)
-    if scaled:
-        rows = rows * row_ref[:, :1]
-    send_ref[...] = rows.astype(BF).reshape(send_ref.shape)
+    heads = HEAD // CAP
+    for sel_ref, row_ref, first, last, span in (
+        (head_ref, head_row, 0, heads, pl.ds(0, HEAD)),
+        (tail_ref, tail_row, heads, blocks, pl.ds(HEAD, packed - HEAD)),
+    ):
+        stack = jnp.concatenate(
+            [wide[:, q * BLK : (q + 1) * BLK] for q in range(first, last)], axis=0
+        )
+        rows = dot_nn(sel_ref[...], stack)
+        if scaled:
+            rows = rows * row_ref[:, :1]
+        send_ref[:, 0, span, :] = rows.astype(BF).reshape(N_Z, -1, BLK)
 
 
 def packed_rows(width):
@@ -162,8 +178,10 @@
             + [seg_spec(k) for k in range(N_X)],
             out_specs=out_specs,
             scratch_shapes=[
-                pltpu.VMEM((total, blocks * tok), BF),
-                pltpu.VMEM((total, 128), F32),
+                pltpu.VMEM((N_Z * HEAD, HEAD // CAP * tok), BF),
+                pltpu.VMEM((total - N_Z * HEAD, (blocks - HEAD // CAP) * tok), BF),
+                pltpu.VMEM((N_Z * HEAD, 128), F32),
+                pltpu.VMEM((total - N_Z * HEAD, 128), F32),
             ],
         ),
         out_shape=out_shape,
@@ -178,14 +196,18 @@
 
 def unpack_kernel(in_ref, out_ref):
     packed = in_ref.shape[1]
-    blocks = packed // CAP
-    row, col = iota((blocks * GROWS, 1), 0), iota((1, N_Z * packed), 1)
-    place = row % GROWS
-    want = place // CAP * packed + row // GROWS * CAP + place % CAP
-    perm = jnp.where(col == want, 1.0, 0.0).astype(BF)
-    out = dot_nn(perm, in_ref[...].reshape(N_Z * packed, BLK))
-    for q in range(blocks):
-        out_ref[:, pl.ds(q * BLK, BLK)] = out[q * GROWS : (q + 1) * GROWS].astype(BF)
+    heads = HEAD // CAP
+    groups = ((0, heads, 0, HEAD), (heads, packed // CAP, HEAD, packed))
+    for first, last, low, high in groups:
+        count = high - low
+        row, col = iota(((last - first) * GROWS, 1), 0), iota((1, N_Z * count), 1)
+        place = row % GROWS
+        want = place // CAP * count + row // GROWS * CAP + place % CAP
+        perm = jnp.where(col == want, 1.0, 0.0).astype(BF)
+        out = dot_nn(perm, in_ref[:, low:high, :].reshape(N_Z * count, BLK))
+        for q in range(last - first):
+            cols = pl.ds((first + q) * BLK, BLK)
+            out_ref[:, cols] = out[q * GROWS : (q + 1) * GROWS].astype(BF)
 
 
 def unpack(packed):
@@ -208,14 +230,19 @@
     packed = send_ref.shape[1]
     blocks = packed // CAP
     total = sum(r[...].astype(F32) for r in parts)
-    stack = jnp.concatenate(
-        [total[:, q * BLK : (q + 1) * BLK] for q in range(blocks)], axis=0
-    ).astype(BF)
-    row, col = iota((N_Z * packed, 1), 0), iota((1, blocks * GROWS), 1)
-    r = row % packed
-    want = r // CAP * GROWS + row // packed * CAP + r % CAP
-    perm = jnp.where(col == jnp.where(r < blocks * CAP, want, -1), 1.0, 0.0).astype(BF)
-    send_ref[...] = dot_nn(perm, stack).astype(BF).reshape(send_ref.shape)
+    heads = HEAD // CAP
+    groups = ((0, heads, 0, HEAD), (heads, blocks, HEAD, packed))
+    for first, last, low, high in groups:
+        count = high - low
+        stack = jnp.concatenate(
+            [total[:, q * BLK : (q + 1) * BLK] for q in range(first, last)], axis=0
+        ).astype(BF)
+        row, col = iota((N_Z * count, 1), 0), iota((1, (last - first) * GROWS), 1)
+        r = row % count
+        want = r // CAP * GROWS + row // count * CAP + r % CAP
+        valid = r < (last - first) * CAP
+        perm = jnp.where(col == jnp.where(valid, want, -1), 1.0, 0.0).astype(BF)
+        send_ref[:, low:high, :] = dot_nn(perm, stack).astype(BF).reshape(N_Z, count, BLK)
 
 
 def pack(*parts):

time: 192 us -> 190 us (0.990)
  Pallas kernels: 62 us -> 58.7 us
  transfers between devices with their start and end apart: 31 -> 31, of which waited for: 10 -> 10; matrix products, arithmetic and copies ran while one was open for 3% -> 3% of each run, Pallas kernels for 30% -> 29%
where the time goes in v2:
time: 190 us; the launch traced here: 189 us
  starting transfers between devices  68.2 us (36%)
  Pallas kernels  58.7 us (31%)
  waiting for transfers between devices  53.7 us (28%)
  other arithmetic  5.76 us (3%)
    all_to_all x4, starting transfers between devices, exchange(): lax.all_to_all(blocks, ('z', 'c'), split_axis=0, concat_axis=0, tiled=True)  27.4 us
    ppermute x12, waiting for transfers between devices, shift(): return lax.ppermute(a, axis, [(i, (i + step) % n) for i in range(n)])  25.5 us
    ppermute x10, waiting for transfers between devices, swap(): lax.ppermute(a, axis, [(i, i ^ bits) for i in range(lax.axis_size(axis))])  17.4 us
    ppermute x12, starting transfers between devices, shift(): return lax.ppermute(a, axis, [(i, (i + step) % n) for i in range(n)])  16 us
    ppermute x10, starting transfers between devices, swap(): lax.ppermute(a, axis, [(i, i ^ bits) for i in range(lax.axis_size(axis))])  14.4 us
    all_to_all x4, waiting for transfers between devices, exchange(): lax.all_to_all(blocks, ('z', 'c'), split_axis=0, concat_axis=0, tiled=True)  10.7 us
    ppermute x5, starting transfers between devices, swap_core(): return lax.ppermute(a, 'c', [(0, 1), (1, 0)])  10.5 us
    pallas_call x2, Pallas kernels, combine(): pl.pallas_call(combine_kernel, grid_spec=pltpu.PrefetchScalarGridSpec(num...  10.1 us
  transfers between devices with their start and end apart: 31, of which 10 were waited for; matrix products, arithmetic and copies ran while one was open for 3% of the time, Pallas kernels for 29%

profile of v2, /device:TPU:1, one launch (start us, length us, event | category | flops | bytes accessed | tf_op | source)
XLA Modules:
  0.0 188.9 jit_solution(3800343328600492966)
XLA Ops:
  0.6 3.7 %select_tok.1 = (bf16[8,2,72,256]{3,2,1,0:T(8,128)(2,1)}, bf16[128,576]{1,0:T(8,128)(2,1)}, bf16[128,576]{1,0:T(8,128)(2,1)}) custom-call(s32[1]{0:T(128)} %bitcast.x_ref, s32[8,128]{1,0:T(8,128)} %bitcast.25, f32[8,128]{1,0:T(8,128)} %bitcast.27, bf16[128,7168]{1,0:T(8,128)(2,1)} %refs_3_.1, bf16[128,7168]{1,0:T(8,128)(2,1)} %refs_3_.1, ...), custom_call_target="tpu_custom_call" | custom-call | flops 99999997952 | bytes 100000000 | tf_op jit(solution)/shard_map/select_tok/pallas_call | solution.py:169
  4.3 10.0 %all-to-all-start = ((bf16[16,72,256]{2,1,0:T(8,128)(2,1)}), bf16[16,72,256]{2,1,0:T(8,128)(2,1)}, u32[]{:S(2)}, u32[]{:S(2)}) async-start(bf16[16,72,256]{2,1,0:T(8,128)(2,1)} %bitcast.24), calls=%async_computation | async-start | bytes 1179648 | tf_op jit(solution)/shard_map/all_to_all | solution.py:653
  14.3 3.3 %select_cot.1 = bf16[8,2,72,256]{3,2,1,0:T(8,128)(2,1)} custom-call(s32[1]{0:T(128)} %bitcast.x_ref, s32[8,128]{1,0:T(8,128)} %bitcast.26, f32[8,128]{1,0:T(8,128)} %bitcast.28, bf16[128,7168]{1,0:T(8,128)(2,1)} %refs_3_.2, bf16[128,7168]{1,0:T(8,128)(2,1)} %refs_3_.2, bf16[128,7168]{1,0:T(8,128)(2,1)} %refs_3_.2, bf16[128,7168]{1,0:T(8,128)(2,1)} %refs_3_.2), custom_call_target="tpu_custom_call" | custom-call | flops 99999997952 | bytes 100000000 | tf_op jit(solution)/shard_map/select_cot/pallas_call | solution.py:169
  25.9 7.1 %all-to-all-done.in_ref = bf16[16,72,256]{2,1,0:T(8,128)(2,1)} async-done(((bf16[16,72,256]{2,1,0:T(8,128)(2,1)}), bf16[16,72,256]{2,1,0:T(8,128)(2,1)}, u32[]{:S(2)}, u32[]{:S(2)}) %all-to-all-start) | async-done | bytes 589856 | tf_op jit(solution)/shard_map/all_to_all | solution.py:653
  33.1 3.5 %all-to-all-start.2 = ((bf16[16,72,256]{2,1,0:T(8,128)(2,1)}), bf16[16,72,256]{2,1,0:T(8,128)(2,1)S(1)}, u32[]{:S(2)}, u32[]{:S(2)}) async-start(bf16[16,72,256]{2,1,0:T(8,128)(2,1)} %bitcast.6), calls=%async_computation.2 | async-start | bytes 1179648 | tf_op jit(solution)/shard_map/all_to_all | solution.py:653
  43.4 10.2 %collective-permute-done.9.refs_11_.refs_7_ = bf16[896,384]{1,0:T(8,128)(2,1)} collective-permute-done((bf16[896,384]{1,0:T(8,128)(2,1)S(1)}, bf16[896,384]{1,0:T(8,128)(2,1)}, u32[]{:S(2)}, u32[]{:S(2)}) %collective-permute-start.9) | collective-permute-done | bytes 688160 | tf_op jit(solution)/shard_map/ppermute | solution.py:28
  60.0 10.7 %collective-permute-done.14.refs_1_.refs_5_ = bf16[80,3584]{1,0:T(8,128)(2,1)S(1)} collective-permute-done((bf16[80,3584]{1,0:T(8,128)(2,1)S(1)}, bf16[80,3584]{1,0:T(8,128)(2,1)S(1)}, u32[]{:S(2)}, u32[]{:S(2)}) %collective-permute-start.14) | collective-permute-done | bytes 573472 | tf_op jit(solution)/shard_map/ppermute | solution.py:33
  70.7 3.5 %collective-permute-start.15 = (bf16[80,3584]{1,0:T(8,128)(2,1)S(1)}, bf16[80,3584]{1,0:T(8,128)(2,1)S(1)}, u32[]{:S(2)}, u32[]{:S(2)}) collective-permute-start(bf16[80,3584]{1,0:T(8,128)(2,1)S(1)} %collective-permute-done.14.refs_1_.refs_5_), channel_id=1, source_target_pairs={{0,6},{2,0},{4,2},{6,4},{1,7},{3,1},{5,3},{7,5},{8,14},{10,8},{12,... | collective-permute-start | bytes 1720328 | tf_op jit(solution)/shard_map/ppermute | solution.py:33
  74.2 4.7 %project_rows.2.half_ref = f32[320,512]{1,0:T(8,128)S(1)} custom-call(bf16[80,3584]{1,0:T(8,128)(2,1)} %unpack_rows.2.refs_0_, bf16[80,3584]{1,0:T(8,128)(2,1)} %collective-permute-done.1.refs_1_, bf16[80,3584]{1,0:T(8,128)(2,1)S(1)} %collective-permute-done.3.refs_2_, bf16[80,3584]{1,0:T(8,128)(2,1)} %collective-permute-done.2.refs_3_, ...), custom_call_target="tpu_custom_call" | custom-call | flops 99999997952 | bytes 100000000 | tf_op jit(solution)/shard_map/project_rows/pallas_call | solution.py:411
  79.0 4.8 %collective-permute-start.10 = (f32[320,512]{1,0:T(8,128)S(1)}, f32[320,512]{1,0:T(8,128)S(1)}, u32[]{:S(2)}, u32[]{:S(2)}) collective-permute-start(f32[320,512]{1,0:T(8,128)S(1)} %project_rows.2.half_ref), channel_id=1, source_target_pairs={{0,1},{1,0},{2,3},{3,2},{4,5},{5,4},{6,7},{7,6},{8,9},{9,8},{10,11... | collective-permute-start | bytes 1966088 | tf_op jit(solution)/shard_map/ppermute | solution.py:24
  91.8 3.5 %forward_rows.1 = (bf16[320,256]{1,0:T(8,128)(2,1)S(1)}, bf16[80,3584]{1,0:T(8,128)(2,1)S(1)}, bf16[80,3584]{1,0:T(8,128)(2,1)}, bf16[80,3584]{1,0:T(8,128)(2,1)}, bf16[80,3584]{1,0:T(8,128)(2,1)}) custom-call(f32[320,512]{1,0:T(8,128)S(1)} %project_rows.2.half_ref, f32[320,512]{1,0:T(8,128)S(1)} %collective-permute-done.10.other_ref, ...), custom_call_target="tpu_custom_call" | custom-call | flops 99999997952 | bytes 100000000 | tf_op jit(solution)/shard_map/forward_rows/pallas_call | solution.py:478
  98.3 4.2 %backward_rows.1 = (bf16[320,512]{1,0:T(8,128)(2,1)S(1)}, bf16[80,3584]{1,0:T(8,128)(2,1)S(1)}, bf16[80,3584]{1,0:T(8,128)(2,1)}, bf16[80,3584]{1,0:T(8,128)(2,1)}, bf16[80,3584]{1,0:T(8,128)(2,1)}) custom-call(f32[320,512]{1,0:T(8,128)S(1)} %project_rows.2.half_ref, f32[320,512]{1,0:T(8,128)S(1)} %collective-permute-done.10.other_ref, ...), custom_call_target="tpu_custom_call" | custom-call | flops 99999997952 | bytes 100000000 | tf_op jit(solution)/shard_map/backward_rows/pallas_call | solution.py:478
  102.5 7.2 %weight_grad.1 = (bf16[896,384]{1,0:T(8,128)(2,1)S(1)}, bf16[2,896,384]{2,1,0:T(8,128)(2,1)}, bf16[896,384]{1,0:T(8,128)(2,1)S(1)}, bf16[896,384]{1,0:T(8,128)(2...) custom-call(bf16[320,256]{1,0:T(8,128)(2,1)S(1)} %get-tuple-element.50.hidden_ref, ...), custom_call_target="tpu_custom_call" | custom-call | flops 99999997952 | bytes 100000000 | tf_op jit(solution)/shard_map/weight_grad/pallas_call | solution.py:530
  110.7 3.1 %collective-permute-start.21 = (bf16[2,896,384]{2,1,0:T(8,128)(2,1)}, bf16[2,896,384]{2,1,0:T(8,128)(2,1)}, u32[]{:S(2)}, u32[]{:S(2)}) collective-permute-start(bf16[2,896,384]{2,1,0:T(8,128)(2,1)} %get-tuple-element.55), channel_id=1, source_target_pairs={{0,192},{64,128},{128,64},{192,0},{1,193},{65,129},{129,65},{193,1... | collective-permute-start | bytes 4128776 | tf_op jit(solution)/shard_map/ppermute | solution.py:28
  115.0 9.2 %collective-permute-done.12.refs_2_ = bf16[80,3584]{1,0:T(8,128)(2,1)} collective-permute-done((bf16[80,3584]{1,0:T(8,128)(2,1)}, bf16[80,3584]{1,0:T(8,128)(2,1)}, u32[]{:S(2)}, u32[]{:S(2)}) %collective-permute-start.12) | collective-permute-done | bytes 573472 | tf_op jit(solution)/shard_map/ppermute | solution.py:33
  126.9 3.1 %pack_rows.2 = bf16[16,72,256]{2,1,0:T(8,128)(2,1)} custom-call(bf16[80,3584]{1,0:T(8,128)(2,1)S(1)} %get-tuple-element.44.refs_0_, bf16[80,3584]{1,0:T(8,128)(2,1)} %collective-permute-done.11.refs_1_, bf16[80,3584]{1,0:T(8,128)(2,1)} %collective-permute-done.12.refs_2_, bf16[80,3584]{1,0:T(8,128)(2,1)} %collective-permute-done.13.refs_3_), custom_call_target="tpu_custom_call" | custom-call | flops 99999997952 | bytes 100000000 | tf_op jit(solution)/shard_map/pack_rows/pallas_call | solution.py:251
  130.0 8.9 %all-to-all-start.1 = ((bf16[16,72,256]{2,1,0:T(8,128)(2,1)}), bf16[16,72,256]{2,1,0:T(8,128)(2,1)S(1)}, u32[]{:S(2)}, u32[]{:S(2)}) async-start(bf16[16,72,256]{2,1,0:T(8,128)(2,1)} %pack_rows.2), calls=%async_computation.1 | async-start | bytes 1179648 | tf_op jit(solution)/shard_map/all_to_all | solution.py:653
  138.9 4.8 %collective-permute-done.21 = bf16[2,896,384]{2,1,0:T(8,128)(2,1)} collective-permute-done((bf16[2,896,384]{2,1,0:T(8,128)(2,1)}, bf16[2,896,384]{2,1,0:T(8,128)(2,1)}, u32[]{:S(2)}, u32[]{:S(2)}) %collective-permute-start.21) | collective-permute-done | bytes 1376288 | tf_op jit(solution)/shard_map/ppermute | solution.py:28
  145.9 3.1 %collective-permute-done.19.refs_2_ = bf16[80,3584]{1,0:T(8,128)(2,1)} collective-permute-done((bf16[80,3584]{1,0:T(8,128)(2,1)}, bf16[80,3584]{1,0:T(8,128)(2,1)}, u32[]{:S(2)}, u32[]{:S(2)}) %collective-permute-start.19) | collective-permute-done | bytes 573472 | tf_op jit(solution)/shard_map/ppermute | solution.py:33
  149.0 3.1 %pack_rows.3 = bf16[16,72,256]{2,1,0:T(8,128)(2,1)} custom-call(bf16[80,3584]{1,0:T(8,128)(2,1)S(1)} %copy-done.15, bf16[80,3584]{1,0:T(8,128)(2,1)S(1)} %collective-permute-done.18.refs_1_, bf16[80,3584]{1,0:T(8,128)(2,1)} %collective-permute-done.19.refs_2_, bf16[80,3584]{1,0:T(8,128)(2,1)} %collective-permute-done.20.refs_3_), custom_call_target="tpu_custom_call" | custom-call | flops 99999997952 | bytes 100000000 | tf_op jit(solution)/shard_map/pack_rows/pallas_call | solution.py:251
  157.6 5.0 %all-to-all-start.3 = ((bf16[16,72,256]{2,1,0:T(8,128)(2,1)}), bf16[16,72,256]{2,1,0:T(8,128)(2,1)}, u32[]{:S(2)}, u32[]{:S(2)}) async-start(bf16[16,72,256]{2,1,0:T(8,128)(2,1)} %pack_rows.3), calls=%async_computation.3 | async-start | bytes 1179648 | tf_op jit(solution)/shard_map/all_to_all | solution.py:653
  165.5 4.4 %combine_rows.2 = bf16[128,7168]{1,0:T(8,128)(2,1)} custom-call(s32[1]{0:T(128)} %bitcast.x_ref, bf16[128,576]{1,0:T(8,128)(2,1)S(1)} %copy-done.17, bf16[8,2,72,256]{3,2,1,0:T(8,128)(2,1)S(1)} %bitcast.23), custom_call_target="tpu_custom_call" | custom-call | flops 99999997952 | bytes 100000000 | tf_op jit(solution)/shard_map/combine_rows/pallas_call | solution.py:306
  172.3 5.5 %update_master.1 = (bf16[1792,384]{1,0:T(8,128)(2,1)S(1)}, f32[1,3,1792]{2,1,0:T(4,128)S(1)}) custom-call(s32[1]{0:T(128)} %bitcast.4.c_ref, f32[1,1792,384]{2,1,0:T(8,128)S(1)} %copy-done, f32[1,3,1792]{2,1,0:T(4,128)S(1)} %copy.10.sums_ref, bf16[896,384]{1,0:T(8,128)(2,1)S(1)} %collective-permute-done.23.other_ref, bf16[896,384]{1,0:T(8,128)(2,1)S(1)} %copy-done.13, ...), custom_call_target="tpu_custom_call" | custom-call | flops 99999997952 | bytes 100000000 | tf_op jit(solution)/shard_map/update_master/pallas_call | solution.py:617
  181.4 5.7 %combine_rows.3 = bf16[128,7168]{1,0:T(8,128)(2,1)} custom-call(s32[1]{0:T(128)} %bitcast.x_ref, bf16[128,576]{1,0:T(8,128)(2,1)S(1)} %copy-done.16, bf16[8,2,72,256]{3,2,1,0:T(8,128)(2,1)} %bitcast.7.back_ref), custom_call_target="tpu_custom_call" | custom-call | flops 99999997952 | bytes 100000000 | tf_op jit(solution)/shard_map/combine_rows/pallas_call | solution.py:306
  (97 shorter events, 55.5 us)
Async XLA Ops:
  4.3 28.8 %all-to-all-start = ((bf16[16,72,256]{2,1,0:T(8,128)(2,1)}), bf16[16,72,256]{2,1,0:T(8,128)(2,1)}, u32[]{:S(2)}, u32[]{:S(2)}) async-start(bf16[16,72,256]{2,1,0:T(8,128)(2,1)} %bitcast.24), calls=%async_computation | async-start | bytes 1179648 | tf_op jit(solution)/shard_map/all_to_all | solution.py:653
  20.7 22.5 %collective-permute-start.6 = (bf16[896,384]{1,0:T(8,128)(2,1)}, bf16[896,384]{1,0:T(8,128)(2,1)S(1)}, u32[]{:S(2)}, u32[]{:S(2)}) collective-permute-start(bf16[896,384]{1,0:T(8,128)(2,1)} %get-tuple-element.43.refs_4_.refs_0_), channel_id=1, source_target_pairs={{0,192},{64,128},{128,64},{192,0},{1,193},{65,129},{129,65},{193,1... | collective-permute-start | bytes 2064392 | tf_op jit(solution)/shard_map/ppermute | solution.py:28
  23.2 20.2 %collective-permute-start.5 = (bf16[896,384]{1,0:T(8,128)(2,1)S(1)}, bf16[896,384]{1,0:T(8,128)(2,1)S(1)}, u32[]{:S(2)}, u32[]{:S(2)}) collective-permute-start(bf16[896,384]{1,0:T(8,128)(2,1)S(1)} %collective-permute-done.refs_5_.refs_1_), channel_id=1, source_target_pairs={{0,64},{64,0},{128,192},{192,128},{1,65},{65,1},{129,193},{193,129... | collective-permute-start | bytes 2064392 | tf_op jit(solution)/shard_map/ppermute | solution.py:28
  24.1 29.5 %collective-permute-start.9 = (bf16[896,384]{1,0:T(8,128)(2,1)S(1)}, bf16[896,384]{1,0:T(8,128)(2,1)}, u32[]{:S(2)}, u32[]{:S(2)}) collective-permute-start(bf16[896,384]{1,0:T(8,128)(2,1)S(1)} %collective-permute-done.refs_5_.refs_1_), channel_id=1, source_target_pairs={{0,192},{64,128},{128,64},{192,0},{1,193},{65,129},{129,65},{193,1... | collective-permute-start | bytes 2064392 | tf_op jit(solution)/shard_map/ppermute | solution.py:28
  33.1 23.1 %all-to-all-start.2 = ((bf16[16,72,256]{2,1,0:T(8,128)(2,1)}), bf16[16,72,256]{2,1,0:T(8,128)(2,1)S(1)}, u32[]{:S(2)}, u32[]{:S(2)}) async-start(bf16[16,72,256]{2,1,0:T(8,128)(2,1)} %bitcast.6), calls=%async_computation.2 | async-start | bytes 1179648 | tf_op jit(solution)/shard_map/all_to_all | solution.py:653
  39.2 16.9 %collective-permute-start.1 = (bf16[80,3584]{1,0:T(8,128)(2,1)}, bf16[80,3584]{1,0:T(8,128)(2,1)}, u32[]{:S(2)}, u32[]{:S(2)}) collective-permute-start(bf16[80,3584]{1,0:T(8,128)(2,1)} %unpack_rows.2.refs_0_), channel_id=1, source_target_pairs={{0,6},{2,0},{4,2},{6,4},{1,7},{3,1},{5,3},{7,5},{8,14},{10,8},{12,... | collective-permute-start | bytes 1720328 | tf_op jit(solution)/shard_map/ppermute | solution.py:33
  41.9 17.9 %collective-permute-start.4 = (bf16[896,384]{1,0:T(8,128)(2,1)S(1)}, bf16[896,384]{1,0:T(8,128)(2,1)}, u32[]{:S(2)}, u32[]{:S(2)}) collective-permute-start(bf16[896,384]{1,0:T(8,128)(2,1)S(1)} %copy-done.1), channel_id=1, source_target_pairs={{0,64},{64,0},{128,192},{192,128},{1,65},{65,1},{129,193},{193,129... | collective-permute-start | bytes 2064392 | tf_op jit(solution)/shard_map/ppermute | solution.py:28
  43.1 31.0 %collective-permute-start.7 = (bf16[896,384]{1,0:T(8,128)(2,1)S(1)}, bf16[896,384]{1,0:T(8,128)(2,1)}, u32[]{:S(2)}, u32[]{:S(2)}) collective-permute-start(bf16[896,384]{1,0:T(8,128)(2,1)S(1)} %collective-permute-done.6.refs_10_.refs_6_), channel_id=1, source_target_pairs={{0,64},{64,0},{128,192},{192,128},{1,65},{65,1},{129,193},{193,129... | collective-permute-start | bytes 2064392 | tf_op jit(solution)/shard_map/ppermute | solution.py:28
  43.4 16.4 %collective-permute-start.2 = (bf16[80,3584]{1,0:T(8,128)(2,1)}, bf16[80,3584]{1,0:T(8,128)(2,1)}, u32[]{:S(2)}, u32[]{:S(2)}) collective-permute-start(bf16[80,3584]{1,0:T(8,128)(2,1)} %unpack_rows.2.refs_0_), channel_id=1, source_target_pairs={{0,2},{2,4},{4,6},{6,0},{1,3},{3,5},{5,7},{7,1},{8,10},{10,12},{12... | collective-permute-start | bytes 1720328 | tf_op jit(solution)/shard_map/ppermute | solution.py:33
  53.6 20.6 %collective-permute-start.8 = (bf16[896,384]{1,0:T(8,128)(2,1)S(1)}, bf16[896,384]{1,0:T(8,128)(2,1)}, u32[]{:S(2)}, u32[]{:S(2)}) collective-permute-start(bf16[896,384]{1,0:T(8,128)(2,1)S(1)} %collective-permute-done.5.refs_7_.refs_3_), channel_id=1, source_target_pairs={{0,192},{64,128},{128,64},{192,0},{1,193},{65,129},{129,65},{193,1... | collective-permute-start | bytes 2064392 | tf_op jit(solution)/shard_map/ppermute | solution.py:28
  59.9 26.4 %collective-permute-start.16 = (bf16[80,3584]{1,0:T(8,128)(2,1)S(1)}, bf16[80,3584]{1,0:T(8,128)(2,1)S(1)}, u32[]{:S(2)}, u32[]{:S(2)}) collective-permute-start(bf16[80,3584]{1,0:T(8,128)(2,1)S(1)} %unpack_rows.3.refs_0_.refs_4_), channel_id=1, source_target_pairs={{0,2},{2,4},{4,6},{6,0},{1,3},{3,5},{5,7},{7,1},{8,10},{10,12},{12... | collective-permute-start | bytes 1720328 | tf_op jit(solution)/shard_map/ppermute | solution.py:33
  70.7 15.6 %collective-permute-start.15 = (bf16[80,3584]{1,0:T(8,128)(2,1)S(1)}, bf16[80,3584]{1,0:T(8,128)(2,1)S(1)}, u32[]{:S(2)}, u32[]{:S(2)}) collective-permute-start(bf16[80,3584]{1,0:T(8,128)(2,1)S(1)} %collective-permute-done.14.refs_1_.refs_5_), channel_id=1, source_target_pairs={{0,6},{2,0},{4,2},{6,4},{1,7},{3,1},{5,3},{7,5},{8,14},{10,8},{12,... | collective-permute-start | bytes 1720328 | tf_op jit(solution)/shard_map/ppermute | solution.py:33
  95.3 18.6 %collective-permute-start.11 = (bf16[80,3584]{1,0:T(8,128)(2,1)}, bf16[80,3584]{1,0:T(8,128)(2,1)}, u32[]{:S(2)}, u32[]{:S(2)}) collective-permute-start(bf16[80,3584]{1,0:T(8,128)(2,1)} %get-tuple-element.45), channel_id=1, source_target_pairs={{0,4},{2,6},{4,0},{6,2},{1,5},{3,7},{5,1},{7,3},{8,12},{10,14},{12... | collective-permute-start | bytes 1720328 | tf_op jit(solution)/shard_map/ppermute | solution.py:33
  95.6 28.7 %collective-permute-start.12 = (bf16[80,3584]{1,0:T(8,128)(2,1)}, bf16[80,3584]{1,0:T(8,128)(2,1)}, u32[]{:S(2)}, u32[]{:S(2)}) collective-permute-start(bf16[80,3584]{1,0:T(8,128)(2,1)} %get-tuple-element.46), channel_id=1, source_target_pairs={{0,2},{2,4},{4,6},{6,0},{1,3},{3,5},{5,7},{7,1},{8,10},{10,12},{12... | collective-permute-start | bytes 1720328 | tf_op jit(solution)/shard_map/ppermute | solution.py:33
  97.6 26.6 %collective-permute-start.13 = (bf16[80,3584]{1,0:T(8,128)(2,1)}, bf16[80,3584]{1,0:T(8,128)(2,1)}, u32[]{:S(2)}, u32[]{:S(2)}) collective-permute-start(bf16[80,3584]{1,0:T(8,128)(2,1)} %get-tuple-element.47), channel_id=1, source_target_pairs={{0,6},{2,0},{4,2},{6,4},{1,7},{3,1},{5,3},{7,5},{8,14},{10,8},{12,... | collective-permute-start | bytes 1720328 | tf_op jit(solution)/shard_map/ppermute | solution.py:33
  110.7 33.1 %collective-permute-start.21 = (bf16[2,896,384]{2,1,0:T(8,128)(2,1)}, bf16[2,896,384]{2,1,0:T(8,128)(2,1)}, u32[]{:S(2)}, u32[]{:S(2)}) collective-permute-start(bf16[2,896,384]{2,1,0:T(8,128)(2,1)} %get-tuple-element.55), channel_id=1, source_target_pairs={{0,192},{64,128},{128,64},{192,0},{1,193},{65,129},{129,65},{193,1... | collective-permute-start | bytes 4128776 | tf_op jit(solution)/shard_map/ppermute | solution.py:28
  113.8 38.2 %collective-permute-start.24 = (bf16[2,896,384]{2,1,0:T(8,128)(2,1)}, bf16[2,896,384]{2,1,0:T(8,128)(2,1)}, u32[]{:S(2)}, u32[]{:S(2)}) collective-permute-start(bf16[2,896,384]{2,1,0:T(8,128)(2,1)} %get-tuple-element.54), channel_id=1, source_target_pairs={{0,64},{64,0},{128,192},{192,128},{1,65},{65,1},{129,193},{193,129... | collective-permute-start | bytes 4128776 | tf_op jit(solution)/shard_map/ppermute | solution.py:28
  113.8 32.1 %collective-permute-start.18 = (bf16[80,3584]{1,0:T(8,128)(2,1)}, bf16[80,3584]{1,0:T(8,128)(2,1)S(1)}, u32[]{:S(2)}, u32[]{:S(2)}) collective-permute-start(bf16[80,3584]{1,0:T(8,128)(2,1)} %get-tuple-element.58), channel_id=1, source_target_pairs={{0,4},{2,6},{4,0},{6,2},{1,5},{3,7},{5,1},{7,3},{8,12},{10,14},{12... | collective-permute-start | bytes 1720328 | tf_op jit(solution)/shard_map/ppermute | solution.py:33
  124.2 24.8 %collective-permute-start.19 = (bf16[80,3584]{1,0:T(8,128)(2,1)}, bf16[80,3584]{1,0:T(8,128)(2,1)}, u32[]{:S(2)}, u32[]{:S(2)}) collective-permute-start(bf16[80,3584]{1,0:T(8,128)(2,1)} %get-tuple-element.60), channel_id=1, source_target_pairs={{0,2},{2,4},{4,6},{6,0},{1,3},{3,5},{5,7},{7,1},{8,10},{10,12},{12... | collective-permute-start | bytes 1720328 | tf_op jit(solution)/shard_map/ppermute | solution.py:33
  124.2 24.8 %collective-permute-start.20 = (bf16[80,3584]{1,0:T(8,128)(2,1)}, bf16[80,3584]{1,0:T(8,128)(2,1)}, u32[]{:S(2)}, u32[]{:S(2)}) collective-permute-start(bf16[80,3584]{1,0:T(8,128)(2,1)} %get-tuple-element.62), channel_id=1, source_target_pairs={{0,6},{2,0},{4,2},{6,4},{1,7},{3,1},{5,3},{7,5},{8,14},{10,8},{12,... | collective-permute-start | bytes 1720328 | tf_op jit(solution)/shard_map/ppermute | solution.py:33
  130.0 27.6 %all-to-all-start.1 = ((bf16[16,72,256]{2,1,0:T(8,128)(2,1)}), bf16[16,72,256]{2,1,0:T(8,128)(2,1)S(1)}, u32[]{:S(2)}, u32[]{:S(2)}) async-start(bf16[16,72,256]{2,1,0:T(8,128)(2,1)} %pack_rows.2), calls=%async_computation.1 | async-start | bytes 1179648 | tf_op jit(solution)/shard_map/all_to_all | solution.py:653
  145.9 16.7 %collective-permute-start.22 = (bf16[896,384]{1,0:T(8,128)(2,1)}, bf16[896,384]{1,0:T(8,128)(2,1)S(1)}, u32[]{:S(2)}, u32[]{:S(2)}) collective-permute-start(bf16[896,384]{1,0:T(8,128)(2,1)} %fusion.1), channel_id=1, source_target_pairs={{0,64},{64,0},{128,192},{192,128},{1,65},{65,1},{129,193},{193,129... | collective-permute-start | bytes 2064392 | tf_op jit(solution)/shard_map/ppermute | solution.py:28
  154.2 18.0 %collective-permute-start.25 = (bf16[896,384]{1,0:T(8,128)(2,1)}, bf16[896,384]{1,0:T(8,128)(2,1)S(1)}, u32[]{:S(2)}, u32[]{:S(2)}) collective-permute-start(bf16[896,384]{1,0:T(8,128)(2,1)} %fusion), channel_id=1, source_target_pairs={{0,192},{64,128},{128,64},{192,0},{1,193},{65,129},{129,65},{193,1... | collective-permute-start | bytes 2064392 | tf_op jit(solution)/shard_map/ppermute | solution.py:28
  157.6 23.8 %all-to-all-start.3 = ((bf16[16,72,256]{2,1,0:T(8,128)(2,1)}), bf16[16,72,256]{2,1,0:T(8,128)(2,1)}, u32[]{:S(2)}, u32[]{:S(2)}) async-start(bf16[16,72,256]{2,1,0:T(8,128)(2,1)} %pack_rows.3), calls=%async_computation.3 | async-start | bytes 1179648 | tf_op jit(solution)/shard_map/all_to_all | solution.py:653
  (26 other events, 216.9 us)
